TPU v7x, 128 devices: a whole 4x4x4 slice. The times are simulated.
128 devices in a mesh: depth: 32 (over z, y, core), rows: 4 (over x).
Axes of the slice: x: 4, y: 4, z: 4, core: 2. Of those that a mesh axis runs over, the one named last changes fastest.
Arguments:
- populations: float32 [19, 192, 128, 256], P(None, 'depth', 'rows'), may hold values from 0 to 1, as said below
- fluid_mask: int32 [192, 128, 256], P('depth', 'rows'), may hold values from 0 to 1
- tissue_tag: int32 [192, 128, 256], P('depth', 'rows'), may hold values from 0 to 3
- colour_table: float32 [4, 4, 256], replicated, may hold values from 0 to 1
Outputs:
- advanced: float32 [19, 192, 128, 256], P(None, 'depth', 'rows')
- rendered: float32 [4, 512, 512], P(None, ('rows', 'depth'))
Inputs may be any that keep to these rules, and one draw needn't show every extreme that they name: Every site's populations are positive and close to a lattice equilibrium.
All inputs are finite; a program needn't handle non-finite values.
Results may differ from a plain program's by a relative error of at most 0.0003.
Values sent between devices are 32-bit elements; how exact they have to be, the bound alone decides.
A program may use at most 64 MiB of HBM per device.

v0:
```python
import functools

import jax
import jax.numpy as jnp
from jax import lax
from jax.experimental import pallas as pl
from jax.experimental.pallas import tpu as pltpu
from jax.sharding import PartitionSpec as P

F32 = jnp.float32
BF16 = jnp.bfloat16
MESH = pl.DeviceIdType.MESH

VELOCITIES = (
    (0, 0, 0), (1, 0, 0), (-1, 0, 0), (0, 1, 0), (0, -1, 0), (0, 0, 1), (0, 0, -1),
    (1, 1, 0), (-1, -1, 0), (1, -1, 0), (-1, 1, 0),
    (1, 0, 1), (-1, 0, -1), (1, 0, -1), (-1, 0, 1),
    (0, 1, 1), (0, -1, -1), (0, 1, -1), (0, -1, 1),
)
OPPOSITE = (0, 2, 1, 4, 3, 6, 5, 8, 7, 10, 9, 12, 11, 14, 13, 16, 15, 18, 17)
PAIRS = tuple((q, q + 1) for q in range(1, 19, 2))
NU_ZERO = 0.12
NU_INFINITY = 0.02
LAMBDA_TIME = 15.0
POWER_INDEX = 0.3568
TAU_ZERO = 0.8
SPEED_SCALE = 0.04
SHEAR_SCALE = 0.07

ORDER = (16, 6, 12, 13, 17, 3, 7, 10, 15, 5, 11, 14, 18, 4, 8, 9, 0, 1, 2)
POS = tuple(ORDER.index(q) for q in range(19))
UP_Z, DOWN_Z = 8, 0
UP_Y = (4, 5, 6, 7, 8)
DOWN_Y = (12, 13, 14, 15, 0)
WALL = -1e30
WALL_LIMIT = -1e29

NQ, NZL, NYL, NX = 19, 6, 32, 256
ND, NR, NC = 32, 4, 16
IMG = 512


def moments(f):
    sums = [f[a] + f[b] for a, b in PAIRS]
    diffs = [f[a] - f[b] for a, b in PAIRS]
    density = f[0]
    for s in sums:
        density = density + s
    mx = diffs[0] + (diffs[3] + diffs[4]) + (diffs[5] + diffs[6])
    my = diffs[1] + (diffs[3] - diffs[4]) + (diffs[7] + diffs[8])
    mz = diffs[2] + (diffs[5] - diffs[6]) + (diffs[7] - diffs[8])
    return sums, diffs, density, mx, my, mz


def analyse(f):
    sums, diffs, density, mx, my, mz = moments(f)
    inverse = 1.0 / density
    ux, uy, uz = mx * inverse, my * inverse, mz * inverse
    square = ux * ux + uy * uy + uz * uz
    base = 1.0 - 1.5 * square
    projections = (ux, uy, uz, ux + uy, ux - uy, ux + uz, ux - uz, uy + uz, uy - uz)
    scale_axis = density * (2.0 / 18.0)
    scale_diag = density * (2.0 / 36.0)
    even, odd = [], []
    for k, e in enumerate(projections):
        scale = scale_axis if k < 3 else scale_diag
        even.append(sums[k] - scale * (base + 4.5 * (e * e)))
        odd.append(diffs[k] - scale * (3.0 * e))
    pxx = even[0] + (even[3] + even[4]) + (even[5] + even[6])
    pyy = even[1] + (even[3] + even[4]) + (even[7] + even[8])
    pzz = even[2] + (even[5] + even[6]) + (even[7] + even[8])
    pxy = even[3] - even[4]
    pxz = even[5] - even[6]
    pyz = even[7] - even[8]
    contracted = pxx * pxx + pyy * pyy + pzz * pzz + 2.0 * (pxy * pxy + pxz * pxz + pyz * pyz)
    shear = (1.5 / TAU_ZERO) * inverse * jnp.sqrt(2.0 * contracted + 1e-10)
    return density, base, square, even, odd, shear


def collide(f):
    density, base, _, even, odd, shear = analyse(f)
    scaled = LAMBDA_TIME * shear
    factor = jnp.exp(((POWER_INDEX - 1.0) / 2.0) * jnp.log(1.0 + scaled * scaled))
    tau = 3.0 * (NU_INFINITY + (NU_ZERO - NU_INFINITY) * factor) + 0.5
    omega = 1.0 / tau
    half = 0.5 * omega
    out = [None] * 19
    out[0] = f[0] - omega * (f[0] - (density * (1.0 / 3.0)) * base)
    for k, (a, b) in enumerate(PAIRS):
        s, d = half * even[k], half * odd[k]
        out[a] = f[a] - (s + d)
        out[b] = f[b] - (s - d)
    return out


def kernel(
    pops, mask, tag, table, adv, image,
    pbuf, r1, r2, ysend, yrecv, csend, crecv, bins, cbuf, ssend, srecv, wcols, wrows, vbuf,
    acc, xrecv, pieces, gathered, fsend, frecv,
    in_sem, out_sem, hs_sem, hr_sem, c_send_sem, c_recv_sem, x_sem, g_send_sem, g_recv_sem, f_send_sem, f_recv_sem,
):
    d = lax.axis_index("depth")
    r = lax.axis_index("rows")
    core = lax.rem(d, 2)
    chip = d // 2
    up_d, down_d = lax.rem(d + 1, ND), lax.rem(d + ND - 1, ND)
    up_r, down_r = lax.rem(r + 1, NR), lax.rem(r + NR - 1, NR)

    def at(dd, rr):
        return {"depth": dd, "rows": rr}

    loads = [pltpu.make_async_copy(pops.at[:, z], pbuf.at[:, z], in_sem.at[z]) for z in range(NZL)]
    for z in (0, 5, 1, 2, 3, 4):
        loads[z].start()

    barrier = pltpu.get_barrier_semaphore()
    peers = [at(up_d, r), at(down_d, r), at(up_d, up_r), at(up_d, down_r), at(down_d, up_r), at(down_d, down_r)]
    peers += [at(d, lax.rem(r + k, NR)) for k in range(1, NR)]
    peers += [at(lax.rem(d + 2 * k, ND), r) for k in range(1, NC)]
    peers += [at(d + 1 - 2 * core, r)]
    for peer in peers:
        pl.semaphore_signal(barrier, inc=1, device_id=peer, device_id_type=MESH)

    lane = lax.broadcasted_iota(jnp.int32, (8, 128), 1)
    first_lane, last_lane = lane == 0, lane == 127

    jj = lax.broadcasted_iota(jnp.int32, (128, 96), 0).astype(F32)
    yy = lax.broadcasted_iota(jnp.int32, (128, 96), 1)
    yy = (jnp.where(yy >= 48, yy - 48, yy) - 8).astype(F32)
    wcols[...] = jnp.maximum(0.0, 1.0 - jnp.abs((jj + 0.5) * 0.25 - 0.5 - yy)).astype(BF16)

    def fill_rows(b, carry):
        rho = b * 16 + lax.broadcasted_iota(jnp.int32, (16, NX), 0)
        which = rho & 15
        ii = (which >> 2) * 128 + (((rho >> 4) & 15) * 2 + (rho >> 8)) * 4 + (which & 3)
        xx = lax.broadcasted_iota(jnp.int32, (16, NX), 1).astype(F32)
        wt = jnp.maximum(0.0, 1.0 - jnp.abs((ii.astype(F32) + 0.5) * 0.5 - 0.5 - xx))
        wrows[pl.ds(pl.multiple_of(b * 16, 16), 16), :] = wt.astype(BF16)
        return carry

    lax.fori_loop(0, IMG // 16, fill_rows, 0)

    for k in range(4):
        for c in range(4):
            now = [jnp.broadcast_to(table[k, c:c + 1, h * 128:(h + 1) * 128], (8, 128)) for h in range(2)]
            turned = [pltpu.roll(half, 127, 1) for half in now]
            following = (jnp.where(last_lane, turned[1], turned[0]), jnp.where(last_lane, now[1], turned[1]))
            for h in range(2):
                bins[k, c, 0, h] = now[h]
                bins[k, c, 1, h] = following[h]

    def clear(z, carry):
        for c in range(4):
            cbuf[c, z, 0:8, :] = jnp.zeros((8, NX), F32)
            cbuf[c, z, 40:48, :] = jnp.zeros((8, NX), F32)
        return carry

    lax.fori_loop(0, NZL, clear, 0)

    def fluid_tiles(z, t):
        rows = pl.ds(pl.multiple_of(8 * t, 8), 8)
        return [mask[z, rows, h * 128:(h + 1) * 128] > 0 for h in range(2)]

    def store_relaxed(target, z, t, h, fluid, relaxed):
        rows = pl.ds(pl.multiple_of(8 * t + 8, 8), 8)
        for q in range(19):
            target[POS[q], z + 1, h, rows, :] = jnp.where(fluid, relaxed[q], WALL)

    def first_tile(z, t):
        rows = pl.ds(pl.multiple_of(8 * t, 8), 8)
        fluids = fluid_tiles(z, t)
        for h in range(2):
            f = [pbuf[q, z, rows, h * 128:(h + 1) * 128] for q in range(19)]
            store_relaxed(r1, z, t, h, fluids[h], collide(f))

    def arrive(source, z, t):
        own = pl.ds(pl.multiple_of(8 * t + 8, 8), 8)
        out = [[None] * 19, [None] * 19]
        for q in range(19):
            cx, cy, cz = VELOCITIES[q]
            if q == 0:
                for h in range(2):
                    out[h][0] = source[POS[0], z + 1, h, own, :]
                continue
            rows = own if cy == 0 else pl.ds(8 * t + 8 - cy, 8)
            a = [source[POS[q], z + 1 - cz, h, rows, :] for h in range(2)]
            if cx == 1:
                b0, b1 = pltpu.roll(a[0], 1, 1), pltpu.roll(a[1], 1, 1)
                a = [jnp.where(first_lane, WALL, b0), jnp.where(first_lane, b0, b1)]
            elif cx == -1:
                b0, b1 = pltpu.roll(a[0], 127, 1), pltpu.roll(a[1], 127, 1)
                a = [jnp.where(last_lane, b1, b0), jnp.where(last_lane, WALL, b1)]
            for h in range(2):
                back = source[POS[OPPOSITE[q]], z + 1, h, own, :]
                out[h][q] = jnp.where(a[h] > WALL_LIMIT, a[h], back)
        return out

    def second_tile(z, t):
        fluids = fluid_tiles(z, t)
        f = arrive(r1, z, t)
        for h in range(2):
            store_relaxed(r2, z, t, h, fluids[h], collide(f[h]))

    def lookup(c, after, low, upper, tags):
        picked = []
        for k in range(4):
            a = jnp.take_along_axis(bins[k, c, after, 0], low, axis=1, mode="promise_in_bounds")
            b = jnp.take_along_axis(bins[k, c, after, 1], low, axis=1, mode="promise_in_bounds")
            picked.append(jnp.where(upper, b, a))
        return jnp.where(
            tags[0], jnp.where(tags[1], picked[3], picked[2]), jnp.where(tags[1], picked[1], picked[0])
        )

    def third_tile(z, t):
        fluids = fluid_tiles(z, t)
        rows = pl.ds(pl.multiple_of(8 * t, 8), 8)
        padded = pl.ds(pl.multiple_of(8 * t + 8, 8), 8)
        f = arrive(r2, z, t)
        for h in range(2):
            lanes = slice(h * 128, (h + 1) * 128)
            fluid = fluids[h]
            for q in range(19):
                pbuf[q, z, rows, lanes] = jnp.where(fluid, f[h][q], pbuf[q, z, rows, lanes])
            _, _, square, _, _, shear = analyse(f[h])
            speed = jnp.sqrt(square + 1e-12)
            tags = tag[z, rows, lanes]
            tags = (tags >= 2, (tags & 1) == 1)
            place = []
            for value, scale in ((speed, SPEED_SCALE), (shear, SHEAR_SCALE)):
                where = 255.0 * (value / (value + scale))
                where = jnp.where(fluid, where, 0.0)
                bin_number = jnp.clip(where.astype(jnp.int32), 0, 255)
                place.append((where - bin_number.astype(F32), bin_number & 127, bin_number >= 128))
            result = []
            for c in range(4):
                share, low, upper = place[1 if c == 3 else 0]
                here = lookup(c, 0, low, upper, tags)
                after = lookup(c, 1, low, upper, tags)
                result.append(here + share * (after - here))
            coverage = jnp.where(fluid, result[3] * (3.0 / (NZL * ND)), 0.0)
            for c in range(3):
                cbuf[c, z, padded, lanes] = result[c] * coverage
            cbuf[3, z, padded, lanes] = coverage

    def tiles(count, body, z_of, t_of):
        def step(i, carry):
            body(z_of(i), t_of(i))
            return carry

        lax.fori_loop(0, count, step, 0)

    def remote(src, dst, send, recv, target):
        return pltpu.make_async_remote_copy(
            src_ref=src, dst_ref=dst, send_sem=send, recv_sem=recv, device_id=target, device_id_type=MESH
        )

    def halo_copies(s, rel):
        layers = [
            remote(rel.at[UP_Z:UP_Z + 5, 6, :, 8:40, :], rel.at[UP_Z:UP_Z + 5, 0, :, 8:40, :],
                   hs_sem.at[s, 0], hr_sem.at[s, 0], at(up_d, r)),
            remote(rel.at[DOWN_Z:DOWN_Z + 5, 1, :, 8:40, :], rel.at[DOWN_Z:DOWN_Z + 5, 7, :, 8:40, :],
                   hs_sem.at[s, 1], hr_sem.at[s, 1], at(down_d, r)),
        ]
        rows = [
            remote(ysend.at[s, 0], yrecv.at[s, 0], hs_sem.at[s, 2], hr_sem.at[s, 2], at(d, up_r)),
            remote(ysend.at[s, 1], yrecv.at[s, 1], hs_sem.at[s, 3], hr_sem.at[s, 3], at(d, down_r)),
        ]
        corners = [
            remote(csend.at[s, n], crecv.at[s, n], hs_sem.at[s, 4 + n], hr_sem.at[s, 4 + n], at(dd, rr))
            for n, (dd, rr) in enumerate(((up_d, up_r), (down_d, down_r), (down_d, up_r), (up_d, down_r)))
        ]
        return layers, rows, corners

    corner_places = ((15, 6, 39, 0, 7), (16, 1, 8, 7, 40), (17, 1, 39, 7, 7), (18, 6, 8, 0, 40))

    def pack_corners(s, rel):
        for n, (q, layer, row, _, _) in enumerate(corner_places):
            for h in range(2):
                csend[s, n, h:h + 1, :] = rel[POS[q], layer, h, row:row + 1, :]

    def pack_rows(s, rel):
        def step(z, carry):
            for side, (slots, row) in enumerate(((UP_Y, 39), (DOWN_Y, 8))):
                for n, slot in enumerate(slots):
                    for h in range(2):
                        ysend[s, side, z, 2 * n + h:2 * n + h + 1, :] = rel[slot, z + 1, h, row:row + 1, :]
            return carry

        lax.fori_loop(0, NZL, step, 0)

    def unpack_rows(s, rel):
        def step(z, carry):
            for side, (slots, row, edge) in enumerate(((UP_Y, 7, r == 0), (DOWN_Y, 40, r == NR - 1))):
                for n, slot in enumerate(slots):
                    for h in range(2):
                        rel[slot, z + 1, h, row:row + 1, :] = jnp.where(
                            edge, WALL, yrecv[s, side, z, 2 * n + h:2 * n + h + 1, :]
                        )
            return carry

        lax.fori_loop(0, NZL, step, 0)

    def unpack_layers(s, rel):
        @pl.when(d == 0)
        def _():
            rel[UP_Z:UP_Z + 5, 0] = jnp.full((5, 2, 48, 128), WALL, F32)

        @pl.when(d == ND - 1)
        def _():
            rel[DOWN_Z:DOWN_Z + 5, 7] = jnp.full((5, 2, 48, 128), WALL, F32)

        edges = (
            (d == 0) | (r == 0), (d == ND - 1) | (r == NR - 1), (d == ND - 1) | (r == 0), (d == 0) | (r == NR - 1)
        )
        for n, (q, _, _, layer, row) in enumerate(corner_places):
            for h in range(2):
                rel[POS[q], layer, h, row:row + 1, :] = jnp.where(edges[n], WALL, crecv[s, n, h:h + 1, :])

    loads[0].wait()
    loads[5].wait()
    tiles(8, first_tile, lambda i: (i // 4) * 5, lambda i: lax.rem(i, 4))
    pack_corners(0, r1)
    pl.semaphore_wait(barrier, len(peers))
    layers1, rows1, corners1 = halo_copies(0, r1)
    for copy in layers1 + corners1:
        copy.start()
    for z in range(1, 5):
        loads[z].wait()
    tiles(16, first_tile, lambda i: 1 + i // 4, lambda i: lax.rem(i, 4))
    pack_rows(0, r1)
    for copy in rows1:
        copy.start()

    tiles(8, second_tile, lambda i: 1 + i // 2, lambda i: 1 + lax.rem(i, 2))
    for copy in rows1:
        copy.wait()
    unpack_rows(0, r1)
    tiles(8, second_tile, lambda i: 1 + i // 2, lambda i: 3 * lax.rem(i, 2))
    for copy in layers1 + corners1:
        copy.wait()
    unpack_layers(0, r1)
    tiles(8, second_tile, lambda i: (i // 4) * 5, lambda i: lax.rem(i, 4))
    layers2, rows2, corners2 = halo_copies(1, r2)
    pack_corners(1, r2)
    for copy in layers2 + corners2:
        copy.start()
    pack_rows(1, r2)
    for copy in rows2:
        copy.start()

    tiles(8, third_tile, lambda i: 1 + i // 2, lambda i: 1 + lax.rem(i, 2))
    for copy in rows2:
        copy.wait()
    unpack_rows(1, r2)
    tiles(8, third_tile, lambda i: 1 + i // 2, lambda i: 3 * lax.rem(i, 2))
    for copy in layers2 + corners2:
        copy.wait()
    unpack_layers(1, r2)
    tiles(8, third_tile, lambda i: (i // 4) * 5, lambda i: lax.rem(i, 4))
    stores = [pltpu.make_async_copy(pbuf.at[:, z], adv.at[:, z], out_sem.at[z]) for z in range(NZL)]
    for copy in stores:
        copy.start()

    site_copies = []
    for side, row in enumerate((39, 8)):
        for z in range(NZL):
            for c in range(4):
                place = (z % 2) * 4 + c
                ssend[side, z // 2, place:place + 1, :] = cbuf[c, z, row:row + 1, :]
    for side, target in enumerate((at(d, up_r), at(d, down_r))):
        site_copies.append(remote(ssend.at[side], srecv.at[side], c_send_sem.at[side], c_recv_sem.at[side], target))
        site_copies[-1].start()
    for copy in site_copies:
        copy.wait()
    for side, (row, edge) in enumerate(((7, r == 0), (40, r == NR - 1))):
        for z in range(NZL):
            for c in range(4):
                place = (z % 2) * 4 + c
                cbuf[c, z, row:row + 1, :] = jnp.where(edge, 0.0, srecv[side, z // 2, place:place + 1, :])

    def columns(z, carry):
        for c in range(4):
            sites = cbuf[c, z]
            high = sites.astype(BF16)
            low = (sites - high.astype(F32)).astype(BF16)
            wide = lax.dot_general(
                wcols[...], jnp.concatenate([high, low], axis=0), (((1,), (0,)), ((), ())),
                preferred_element_type=F32,
            )
            high = wide.astype(BF16)
            low = (wide - high.astype(F32)).astype(BF16)
            place = slice((c % 2) * 128, (c % 2) * 128 + 128)
            vbuf[z, c // 2, 0, place, :] = high
            vbuf[z, c // 2, 1, place, :] = low
        return carry

    lax.fori_loop(0, NZL, columns, 0)

    def render(slot, which):
        weights = wrows[pl.ds(pl.multiple_of(which * 256, 256), 256), :]
        acc[slot] = jnp.zeros((4, 256, 128), F32)

        def layer(z, carry):
            drawn = []
            for pair in range(2):
                parts = [
                    lax.dot_general(
                        weights, vbuf[z, pair, n], (((1,), (1,)), ((), ())), preferred_element_type=F32
                    )
                    for n in range(2)
                ]
                drawn.append(parts[0] + parts[1])
            through = 1.0 - acc[slot, 3]
            for c in range(4):
                part = drawn[c // 2][:, (c % 2) * 128:(c % 2) * 128 + 128]
                acc[slot, c] = acc[slot, c] + through * part
            return carry

        lax.fori_loop(0, NZL, layer, 0)

    partner = at(d + 1 - 2 * core, r)
    render(0, 1 - core)
    swap = remote(acc.at[0], xrecv, x_sem.at[0], x_sem.at[1], partner)
    swap.start()
    render(1, core)
    swap.wait()

    def join(n, carry):
        rows = pl.ds(pl.multiple_of(n * 16, 16), 16)
        front = core == 0
        mine = [acc[1, c, rows, :] for c in range(4)]
        theirs = [xrecv[c, rows, :] for c in range(4)]
        near = [jnp.where(front, mine[c], theirs[c]) for c in range(4)]
        far = [jnp.where(front, theirs[c], mine[c]) for c in range(4)]
        through = 1.0 - near[3]
        for c in range(4):
            pieces[n, c] = near[c] + through * far[c]
        return carry

    lax.fori_loop(0, NC, join, 0)

    exchange = []
    for k in range(1, NC):
        other = lax.rem(chip + k, NC)
        exchange.append(
            remote(pieces.at[other], gathered.at[chip], g_send_sem.at[k], g_recv_sem.at[k], at(2 * other + core, r))
        )
        exchange[-1].start()
    gathered[chip] = pieces[chip]
    for copy in exchange:
        copy.wait()

    def over(n, carry):
        through = 1.0 - carry[3]
        return tuple(carry[c] + through * gathered[n, c] for c in range(4))

    final = lax.fori_loop(1, NC, over, tuple(gathered[0, c] for c in range(4)))

    for rr in range(NR):
        for c in range(4):
            fsend[rr, 4 * c:4 * c + 4, :] = final[c][4 * rr:4 * rr + 4, :]
    last = []
    for k in range(1, NR):
        other = lax.rem(r + k, NR)
        last.append(remote(fsend.at[other], frecv.at[r], f_send_sem.at[k], f_recv_sem.at[k], at(d, other)))
        last[-1].start()
    frecv[r] = fsend[r]
    for copy in last:
        copy.wait()
    for rr in range(NR):
        for c in range(4):
            image[c, :, rr * 128:(rr + 1) * 128] = frecv[rr, 4 * c:4 * c + 4, :]
    for copy in stores:
        copy.wait()


def shards(populations, fluid_mask, tissue_tag, colour_table):
    dma = pltpu.SemaphoreType.DMA
    vmem = pl.BlockSpec(memory_space=pltpu.VMEM)
    anywhere = pl.BlockSpec(memory_space=pl.ANY)
    return pl.pallas_call(
        kernel,
        out_shape=(
            jax.ShapeDtypeStruct(populations.shape, F32),
            jax.ShapeDtypeStruct((4, IMG // (ND * NR), IMG), F32),
        ),
        in_specs=[anywhere, vmem, vmem, vmem],
        out_specs=(anywhere, vmem),
        scratch_shapes=[
            pltpu.VMEM((NQ, NZL, NYL, NX), F32),
            pltpu.VMEM((NQ, NZL + 2, 2, 48, 128), F32),
            pltpu.VMEM((NQ, NZL + 2, 2, 48, 128), F32),
            pltpu.VMEM((2, 2, NZL, 16, 128), F32),
            pltpu.VMEM((2, 2, NZL, 16, 128), F32),
            pltpu.VMEM((2, 4, 8, 128), F32),
            pltpu.VMEM((2, 4, 8, 128), F32),
            pltpu.VMEM((4, 4, 2, 2, 8, 128), F32),
            pltpu.VMEM((4, NZL, 48, NX), F32),
            pltpu.VMEM((2, 3, 8, NX), F32),
            pltpu.VMEM((2, 3, 8, NX), F32),
            pltpu.VMEM((128, 96), BF16),
            pltpu.VMEM((IMG, NX), BF16),
            pltpu.VMEM((NZL, 2, 2, 256, NX), BF16),
            pltpu.VMEM((2, 4, 256, 128), F32),
            pltpu.VMEM((4, 256, 128), F32),
            pltpu.VMEM((NC, 4, 16, 128), F32),
            pltpu.VMEM((NC, 4, 16, 128), F32),
            pltpu.VMEM((NR, 16, 128), F32),
            pltpu.VMEM((NR, 16, 128), F32),
            dma((NZL,)), dma((NZL,)), dma((2, 8)), dma((2, 8)), dma((2,)), dma((2,)), dma((2,)),
            dma((NC,)), dma((NC,)), dma((NR,)), dma((NR,)),
        ],
        compiler_params=pltpu.CompilerParams(
            collective_id=0, has_side_effects=True, vmem_limit_bytes=56 * 2**20
        ),
        name="vessel",
    )(populations, fluid_mask, tissue_tag, colour_table)


def solution(mesh):
    placed = (
        P(None, "depth", "rows", None),
        P("depth", "rows", None),
        P("depth", "rows", None),
        P(),
    )
    return jax.shard_map(
        shards,
        mesh=mesh,
        in_specs=placed,
        out_specs=(P(None, "depth", "rows", None), P(None, ("rows", "depth"), None)),
        check_vma=False,
    )
```

profile of v0, /device:TPU:0, one launch (start us, length us, event | category | flops | bytes accessed | tf_op | source)
XLA Modules:
  0.0 55.3 jit_solution(10150497958965076572)
XLA Ops:
  0.6 49.6 %vessel.1 = (f32[19,6,32,256]{3,2,1,0:T(8,128)}, f32[4,4,512]{2,1,0:T(4,128)}) custom-call(f32[19,6,32,256]{3,2,1,0:T(8,128)} %pops.1, s32[6,32,256]{2,1,0:T(8,128)} %mask.1, s32[6,32,256]{2,1,0:T(8,128)} %tag.1, f32[4,4,256]{2,1,0:T(4,128)} %table.1), custom_call_target="tpu_custom_call" | custom-call | tf_op jit(solution)/shard_map/vessel/pallas_call | solution.py:481
  50.2 0.0 copy-start
  50.2 4.4 %copy.8 = f32[19,6,32,256]{3,2,1,0:T(8,128)} copy(f32[19,6,32,256]{3,2,1,0:T(8,128)} %get-tuple-element.4) | data formatting | bytes 7471104
  54.7 0.0 copy-done
  54.7 0.6 %copy.9 = f32[4,4,512]{2,1,0:T(4,128)} copy(f32[4,4,512]{2,1,0:T(4,128)S(1)} %copy-done) | data formatting | bytes 65536
Async XLA Ops:
  50.2 4.4 %copy-start = (f32[4,4,512]{2,1,0:T(4,128)S(1)}, f32[4,4,512]{2,1,0:T(4,128)}, u32[]{:S(2)}) copy-start(f32[4,4,512]{2,1,0:T(4,128)} %get-tuple-element.5) | copy-start | bytes 98308
where the time goes:
time: 55.4 us; the launch traced here: 55.3 us
  Pallas kernels  49.6 us (90%)
  local copies, waits for them, and re-layouts  5.05 us (9%)
  between operations  0.65 us (1%)
    pallas_call x1, Pallas kernels, shards(): pl.pallas_call(kernel, out_shape=(jax.ShapeDtypeStruct(populations.shape,...  49.6 us
    unnamed x4, local copies, waits for them, and re-layouts  5.05 us

commit v1 on v0

v1 whole, which is shorter than its diff:
```python
import functools

import jax
import jax.numpy as jnp
from jax import lax
from jax.experimental import pallas as pl
from jax.experimental.pallas import tpu as pltpu
from jax.sharding import PartitionSpec as P

F32 = jnp.float32
BF16 = jnp.bfloat16
MESH = pl.DeviceIdType.MESH

VELOCITIES = (
    (0, 0, 0), (1, 0, 0), (-1, 0, 0), (0, 1, 0), (0, -1, 0), (0, 0, 1), (0, 0, -1),
    (1, 1, 0), (-1, -1, 0), (1, -1, 0), (-1, 1, 0),
    (1, 0, 1), (-1, 0, -1), (1, 0, -1), (-1, 0, 1),
    (0, 1, 1), (0, -1, -1), (0, 1, -1), (0, -1, 1),
)
OPPOSITE = (0, 2, 1, 4, 3, 6, 5, 8, 7, 10, 9, 12, 11, 14, 13, 16, 15, 18, 17)
PAIRS = tuple((q, q + 1) for q in range(1, 19, 2))
NU_ZERO = 0.12
NU_INFINITY = 0.02
LAMBDA_TIME = 15.0
POWER_INDEX = 0.3568
TAU_ZERO = 0.8
SPEED_SCALE = 0.04
SHEAR_SCALE = 0.07

ORDER = (16, 6, 12, 13, 17, 3, 7, 10, 15, 5, 11, 14, 18, 4, 8, 9, 0, 1, 2)
POS = tuple(ORDER.index(q) for q in range(19))
UP_Z, DOWN_Z = 8, 0
UP_Y = (4, 5, 6, 7, 8)
DOWN_Y = (12, 13, 14, 15, 0)
WALL = -1e30
WALL_REST = (-1e8, -1e12)
LIMIT = -1e5

NQ, NZL, NYL, NX = 19, 6, 32, 256
ND, NR, NC = 32, 4, 16
IMG = 512


def analyse(f, fluid=None, wall=None):
    sums = [f[a] + f[b] for a, b in PAIRS]
    diffs = [f[a] - f[b] for a, b in PAIRS]
    density = ((f[0] + sums[0]) + (sums[1] + sums[2])) + (
        ((sums[3] + sums[4]) + (sums[5] + sums[6])) + (sums[7] + sums[8])
    )
    mx = diffs[0] + ((diffs[3] + diffs[4]) + (diffs[5] + diffs[6]))
    my = diffs[1] + ((diffs[3] - diffs[4]) + (diffs[7] + diffs[8]))
    mz = diffs[2] + ((diffs[5] - diffs[6]) + (diffs[7] - diffs[8]))
    inverse = 1.0 / density
    third = (mx * (1.0 / 3.0), my * (1.0 / 3.0), mz * (1.0 / 3.0))
    hx, hy, hz = (0.5 * q for q in third)
    squares = [q * q for q in third]
    total = squares[0] + squares[1] + squares[2]
    axis_scale = 4.5 * inverse
    diag_scale = 9.0 * inverse
    rest = density - 3.0 * (total * axis_scale)
    if wall is not None:
        rest = jnp.where(fluid, rest, wall)
    axis_rest, diag_rest = rest * (1.0 / 9.0), rest * (1.0 / 18.0)
    diag = (hx + hy, hx - hy, hx + hz, hx - hz, hy + hz, hy - hz)
    even = [(sums[k] - axis_rest) - axis_scale * squares[k] for k in range(3)]
    even += [(sums[3 + k] - diag_rest) - diag_scale * (diag[k] * diag[k]) for k in range(6)]
    odd = [diffs[k] - third[k] for k in range(3)] + [diffs[3 + k] - diag[k] for k in range(6)]
    pxx = even[0] + ((even[3] + even[4]) + (even[5] + even[6]))
    pyy = even[1] + ((even[3] + even[4]) + (even[7] + even[8]))
    pzz = even[2] + ((even[5] + even[6]) + (even[7] + even[8]))
    pxy = even[3] - even[4]
    pxz = even[5] - even[6]
    pyz = even[7] - even[8]
    contracted = (pxx * pxx + pyy * pyy + pzz * pzz) + 2.0 * (pxy * pxy + pxz * pxz + pyz * pyz)
    return inverse, total, rest, even, odd, 2.0 * contracted + 1e-10


def collide(f, fluid, wall):
    inverse, _, rest, even, odd, stress = analyse(f, fluid, wall)
    squared = ((LAMBDA_TIME * 1.5 / TAU_ZERO) ** 2) * ((inverse * inverse) * stress)
    factor = jnp.exp(((POWER_INDEX - 1.0) / 2.0) * jnp.log(1.0 + squared))
    half = 1.0 / ((6.0 * NU_INFINITY + 1.0) + (6.0 * (NU_ZERO - NU_INFINITY)) * factor)
    out = [None] * 19
    out[0] = f[0] - (half + half) * (f[0] - rest * (1.0 / 3.0))
    for k, (a, b) in enumerate(PAIRS):
        s, d = half * even[k], half * odd[k]
        out[a] = f[a] - (s + d)
        out[b] = f[b] - (s - d)
    return out


def diagnose(f):
    inverse, total, _, _, _, stress = analyse(f)
    square = (9.0 * total) * (inverse * inverse) + 1e-12
    speed = square * lax.rsqrt(square)
    shear = (1.5 / TAU_ZERO) * inverse * (stress * lax.rsqrt(stress))
    return speed, shear


def kernel(
    pops, mask_in, tag_in, table, pbuf, image,
    mask, tag, r1, r2, ysend, yrecv, csend, crecv, bins, cbuf, ssend, srecv, wcols, wrows, vbuf,
    acc, xrecv, pieces, gathered, fsend, frecv,
    in_sem, hs_sem, hr_sem, c_send_sem, c_recv_sem, x_sem, g_send_sem, g_recv_sem, f_send_sem, f_recv_sem,
):
    d = lax.axis_index("depth")
    r = lax.axis_index("rows")
    core = lax.rem(d, 2)
    chip = d // 2
    up_d, down_d = lax.rem(d + 1, ND), lax.rem(d + ND - 1, ND)
    up_r, down_r = lax.rem(r + 1, NR), lax.rem(r + NR - 1, NR)

    def at(dd, rr):
        return {"depth": dd, "rows": rr}

    barrier = pltpu.get_barrier_semaphore()
    peers = [at(up_d, r), at(down_d, r), at(up_d, up_r), at(up_d, down_r), at(down_d, up_r), at(down_d, down_r)]
    peers += [at(d, lax.rem(r + k, NR)) for k in range(1, NR)]
    peers += [at(lax.rem(d + 2 * k, ND), r) for k in range(1, NC)]
    peers += [at(d + 1 - 2 * core, r)]
    for peer in peers:
        pl.semaphore_signal(barrier, inc=1, device_id=peer, device_id_type=MESH)

    loads = [pltpu.make_async_copy(pops.at[:, z], pbuf.at[:, z], in_sem.at[z]) for z in range(NZL)]
    loads.append(pltpu.make_async_copy(mask_in, mask, in_sem.at[NZL]))
    loads.append(pltpu.make_async_copy(tag_in, tag, in_sem.at[NZL + 1]))
    for n in (NZL, 0, 5, 1, 2, 3, 4, NZL + 1):
        loads[n].start()

    lane = lax.broadcasted_iota(jnp.int32, (8, 128), 1)
    first_lane, last_lane = lane == 0, lane == 127
    first_limit = jnp.where(first_lane, 1e30, LIMIT)
    last_limit = jnp.where(last_lane, 1e30, LIMIT)

    jj = lax.broadcasted_iota(jnp.int32, (128, 96), 0).astype(F32)
    yy = lax.broadcasted_iota(jnp.int32, (128, 96), 1)
    yy = (jnp.where(yy >= 48, yy - 48, yy) - 8).astype(F32)
    wcols[...] = jnp.maximum(0.0, 1.0 - jnp.abs((jj + 0.5) * 0.25 - 0.5 - yy)).astype(BF16)

    def fill_rows(b, carry):
        rho = b * 64 + lax.broadcasted_iota(jnp.int32, (64, 128), 0)
        ii = (
            (rho >> 8) * 256 + ((rho >> 2) & 1) * 128 + ((rho >> 3) & 15) * 8 + ((rho >> 7) & 1) * 4 + (rho & 3)
        ).astype(F32)
        centre = ii * 0.5 - 0.25
        for h in range(2):
            xx = (lax.broadcasted_iota(jnp.int32, (64, 128), 1) + h * 128).astype(F32)
            wt = jnp.maximum(0.0, 1.0 - jnp.abs(centre - xx)).astype(BF16)
            rows = pl.ds(pl.multiple_of(b * 64, 64), 64)
            wrows[rows, h * 128:(h + 1) * 128] = wt
            wrows[rows, 256 + h * 128:256 + (h + 1) * 128] = wt
        return carry

    lax.fori_loop(0, IMG // 64, fill_rows, 0)

    for k in range(4):
        for c in range(4):
            now = [jnp.broadcast_to(table[k, c:c + 1, h * 128:(h + 1) * 128], (8, 128)) for h in range(2)]
            turned = [pltpu.roll(half, 127, 1) for half in now]
            following = (jnp.where(last_lane, turned[1], turned[0]), jnp.where(last_lane, now[1], turned[1]))
            for h in range(2):
                bins[k, c, 0, h] = now[h]
                bins[k, c, 1, h] = following[h]

    def clear(z, carry):
        for c in range(4):
            cbuf[c, z, 0:8, :] = jnp.zeros((8, NX), F32)
            cbuf[c, z, 40:48, :] = jnp.zeros((8, NX), F32)
        return carry

    lax.fori_loop(0, NZL, clear, 0)

    def fluid_tiles(z, t):
        rows = pl.ds(pl.multiple_of(8 * t, 8), 8)
        return [mask[z, rows, h * 128:(h + 1) * 128] > 0 for h in range(2)]

    def store_relaxed(target, z, t, h, relaxed):
        rows = pl.ds(pl.multiple_of(8 * t + 8, 8), 8)
        for q in range(19):
            target[POS[q], z + 1, h, rows, :] = relaxed[q]

    def first_tile(z, t):
        rows = pl.ds(pl.multiple_of(8 * t, 8), 8)
        fluids = fluid_tiles(z, t)
        for h in range(2):
            f = [pbuf[q, z, rows, h * 128:(h + 1) * 128] for q in range(19)]
            store_relaxed(r1, z, t, h, collide(f, fluids[h], WALL_REST[0]))

    def arrive(source, z, t):
        own = pl.ds(pl.multiple_of(8 * t + 8, 8), 8)
        out = [[None] * 19, [None] * 19]
        for q in range(19):
            cx, cy, cz = VELOCITIES[q]
            if q == 0:
                for h in range(2):
                    out[h][0] = source[POS[0], z + 1, h, own, :]
                continue
            rows = own if cy == 0 else pl.ds(8 * t + 8 - cy, 8)
            a = [source[POS[q], z + 1 - cz, h, rows, :] for h in range(2)]
            limits = [LIMIT, LIMIT]
            if cx == 1:
                b0, b1 = pltpu.roll(a[0], 1, 1), pltpu.roll(a[1], 1, 1)
                a = [b0, jnp.where(first_lane, b0, b1)]
                limits[0] = first_limit
            elif cx == -1:
                b0, b1 = pltpu.roll(a[0], 127, 1), pltpu.roll(a[1], 127, 1)
                a = [jnp.where(last_lane, b1, b0), b1]
                limits[1] = last_limit
            for h in range(2):
                back = source[POS[OPPOSITE[q]], z + 1, h, own, :]
                out[h][q] = jnp.where(a[h] > limits[h], a[h], back)
        return out

    def second_tile(z, t):
        fluids = fluid_tiles(z, t)
        f = arrive(r1, z, t)
        for h in range(2):
            store_relaxed(r2, z, t, h, collide(f[h], fluids[h], WALL_REST[1]))

    def lookup(c, after, low, upper, tags):
        picked = []
        for k in range(4):
            a = jnp.take_along_axis(bins[k, c, after, 0], low, axis=1, mode="promise_in_bounds")
            b = jnp.take_along_axis(bins[k, c, after, 1], low, axis=1, mode="promise_in_bounds")
            picked.append(jnp.where(upper, b, a))
        return jnp.where(
            tags[0], jnp.where(tags[1], picked[3], picked[2]), jnp.where(tags[1], picked[1], picked[0])
        )

    def classify(z, t, places):
        rows = pl.ds(pl.multiple_of(8 * t, 8), 8)
        padded = pl.ds(pl.multiple_of(8 * t + 8, 8), 8)
        fluids = fluid_tiles(z, t)
        for h in range(2):
            lanes = slice(h * 128, (h + 1) * 128)
            tags = tag[z, rows, lanes]
            tags = (tags >= 2, (tags & 1) == 1)
            place = []
            for where in places[2 * h:2 * h + 2]:
                bin_number = jnp.clip(where.astype(jnp.int32), 0, 255)
                place.append((where - bin_number.astype(F32), bin_number & 127, bin_number >= 128))
            result = []
            for c in range(4):
                share, low, upper = place[1 if c == 3 else 0]
                here = lookup(c, 0, low, upper, tags)
                after = lookup(c, 1, low, upper, tags)
                result.append(here + share * (after - here))
            coverage = jnp.where(fluids[h], result[3] * (3.0 / (NZL * ND)), 0.0)
            for c in range(3):
                cbuf[c, z, padded, lanes] = result[c] * coverage
            cbuf[3, z, padded, lanes] = coverage

    def third_tile(z, t):
        fluids = fluid_tiles(z, t)
        rows = pl.ds(pl.multiple_of(8 * t, 8), 8)
        f = arrive(r2, z, t)
        places = []
        for h in range(2):
            lanes = slice(h * 128, (h + 1) * 128)
            for q in range(19):
                pbuf[q, z, rows, lanes] = jnp.where(fluids[h], f[h][q], pbuf[q, z, rows, lanes])
            for value, scale in zip(diagnose(f[h]), (SPEED_SCALE, SHEAR_SCALE)):
                places.append(jnp.where(fluids[h], 255.0 * (value / (value + scale)), 0.0))
        return tuple(places)

    def tiles(count, body, z_of, t_of):
        def step(i, carry):
            body(z_of(i), t_of(i))
            return carry

        lax.fori_loop(0, count, step, 0)

    def remote(src, dst, send, recv, target):
        return pltpu.make_async_remote_copy(
            src_ref=src, dst_ref=dst, send_sem=send, recv_sem=recv, device_id=target, device_id_type=MESH
        )

    def halo_copies(s, rel):
        layers = [
            remote(rel.at[UP_Z:UP_Z + 5, 6, :, 8:40, :], rel.at[UP_Z:UP_Z + 5, 0, :, 8:40, :],
                   hs_sem.at[s, 0], hr_sem.at[s, 0], at(up_d, r)),
            remote(rel.at[DOWN_Z:DOWN_Z + 5, 1, :, 8:40, :], rel.at[DOWN_Z:DOWN_Z + 5, 7, :, 8:40, :],
                   hs_sem.at[s, 1], hr_sem.at[s, 1], at(down_d, r)),
        ]
        rows = [
            remote(ysend.at[s, 0], yrecv.at[s, 0], hs_sem.at[s, 2], hr_sem.at[s, 2], at(d, up_r)),
            remote(ysend.at[s, 1], yrecv.at[s, 1], hs_sem.at[s, 3], hr_sem.at[s, 3], at(d, down_r)),
        ]
        corners = [
            remote(csend.at[s, n], crecv.at[s, n], hs_sem.at[s, 4 + n], hr_sem.at[s, 4 + n], at(dd, rr))
            for n, (dd, rr) in enumerate(((up_d, up_r), (down_d, down_r), (down_d, up_r), (up_d, down_r)))
        ]
        return layers, rows, corners

    corner_places = ((15, 6, 39, 0, 7), (16, 1, 8, 7, 40), (17, 1, 39, 7, 7), (18, 6, 8, 0, 40))

    def pack_corners(s, rel):
        for n, (q, layer, row, _, _) in enumerate(corner_places):
            for h in range(2):
                csend[s, n, h:h + 1, :] = rel[POS[q], layer, h, row:row + 1, :]

    def pack_rows(s, rel):
        def step(z, carry):
            for side, (slots, row) in enumerate(((UP_Y, 39), (DOWN_Y, 8))):
                for n, slot in enumerate(slots):
                    for h in range(2):
                        ysend[s, side, z, 2 * n + h:2 * n + h + 1, :] = rel[slot, z + 1, h, row:row + 1, :]
            return carry

        lax.fori_loop(0, NZL, step, 0)

    def unpack_rows(s, rel):
        def step(z, carry):
            for side, (slots, row, edge) in enumerate(((UP_Y, 7, r == 0), (DOWN_Y, 40, r == NR - 1))):
                for n, slot in enumerate(slots):
                    for h in range(2):
                        rel[slot, z + 1, h, row:row + 1, :] = jnp.where(
                            edge, WALL, yrecv[s, side, z, 2 * n + h:2 * n + h + 1, :]
                        )
            return carry

        lax.fori_loop(0, NZL, step, 0)

    def unpack_layers(s, rel):
        @pl.when(d == 0)
        def _():
            rel[UP_Z:UP_Z + 5, 0] = jnp.full((5, 2, 48, 128), WALL, F32)

        @pl.when(d == ND - 1)
        def _():
            rel[DOWN_Z:DOWN_Z + 5, 7] = jnp.full((5, 2, 48, 128), WALL, F32)

        edges = (
            (d == 0) | (r == 0), (d == ND - 1) | (r == NR - 1), (d == ND - 1) | (r == 0), (d == 0) | (r == NR - 1)
        )
        for n, (q, _, _, layer, row) in enumerate(corner_places):
            for h in range(2):
                rel[POS[q], layer, h, row:row + 1, :] = jnp.where(edges[n], WALL, crecv[s, n, h:h + 1, :])

    loads[NZL].wait()
    loads[0].wait()
    loads[5].wait()
    tiles(8, first_tile, lambda i: (i >> 2) * 5, lambda i: i & 3)
    pack_corners(0, r1)
    pl.semaphore_wait(barrier, len(peers))
    layers1, rows1, corners1 = halo_copies(0, r1)
    for copy in layers1 + corners1:
        copy.start()
    for z in range(1, 5):
        loads[z].wait()
    tiles(16, first_tile, lambda i: 1 + (i >> 2), lambda i: i & 3)
    pack_rows(0, r1)
    for copy in rows1:
        copy.start()

    tiles(8, second_tile, lambda i: 1 + (i >> 1), lambda i: 1 + (i & 1))
    for copy in rows1:
        copy.wait()
    unpack_rows(0, r1)
    tiles(8, second_tile, lambda i: 1 + (i >> 1), lambda i: 3 * (i & 1))
    for copy in layers1 + corners1:
        copy.wait()
    unpack_layers(0, r1)
    tiles(8, second_tile, lambda i: (i >> 2) * 5, lambda i: i & 3)
    layers2, rows2, corners2 = halo_copies(1, r2)
    pack_corners(1, r2)
    for copy in layers2 + corners2:
        copy.start()
    pack_rows(1, r2)
    for copy in rows2:
        copy.start()

    loads[NZL + 1].wait()

    def third_tiles(count, z_of, t_of, before, carry):
        def step(i, places):
            last = jnp.maximum(i - 1, 0)
            first = i == 0
            classify(
                jnp.where(first, before[0], z_of(last)), jnp.where(first, before[1], t_of(last)), places
            )
            return third_tile(z_of(i), t_of(i))

        return lax.fori_loop(0, count, step, carry)

    site_copies = [
        [
            remote(ssend.at[side, 2 * part:3 - (1 - part)], srecv.at[side, 2 * part:3 - (1 - part)], c_send_sem.at[part, side], c_recv_sem.at[part, side], target)
            for side, target in enumerate((at(d, up_r), at(d, down_r)))
        ]
        for part in range(2)
    ]
    places = tuple(jnp.zeros((8, 128), F32) for _ in range(4))
    places = third_tiles(8, lambda i: 1 + (i >> 1), lambda i: 1 + (i & 1), (1, 1), places)
    for copy in rows2:
        copy.wait()
    unpack_rows(1, r2)
    places = third_tiles(8, lambda i: 1 + (i >> 1), lambda i: 3 * (i & 1), (4, 2), places)
    for copy in layers2 + corners2:
        copy.wait()
    unpack_layers(1, r2)
    places = third_tiles(4, lambda i: (i >> 1) * 5, lambda i: 3 * (i & 1), (4, 3), places)

    def pack_sites(part, layers):
        for n, z in enumerate(layers):
            for side, row in enumerate((39, 8)):
                for c in range(4):
                    place = 4 * (n % 2) + c
                    ssend[side, 2 * part + n // 2, place:place + 1, :] = cbuf[c, z, row:row + 1, :]
        for copy in site_copies[part]:
            copy.start()

    def unpack_sites(part, layers):
        for copy in site_copies[part]:
            copy.wait()
        for n, z in enumerate(layers):
            for side, (row, edge) in enumerate(((7, r == 0), (40, r == NR - 1))):
                for c in range(4):
                    place = 4 * (n % 2) + c
                    cbuf[c, z, row:row + 1, :] = jnp.where(
                        edge, 0.0, srecv[side, 2 * part + n // 2, place:place + 1, :]
                    )

    pack_sites(0, (1, 2, 3, 4))
    places = third_tiles(4, lambda i: (i >> 1) * 5, lambda i: 1 + (i & 1), (5, 3), places)
    pack_sites(1, (0, 5))
    classify(5, 2, places)

    def columns(z):
        for c in range(4):
            sites = cbuf[c, z]
            high = sites.astype(BF16)
            low = (sites - high.astype(F32)).astype(BF16)
            wide = lax.dot_general(
                wcols[...], jnp.concatenate([high, low], axis=0), (((1,), (0,)), ((), ())),
                preferred_element_type=F32,
            )
            high = wide.astype(BF16)
            low = (wide - high.astype(F32)).astype(BF16)
            place = slice((c % 2) * 128, (c % 2) * 128 + 128)
            vbuf[z, c // 2, place, 0:NX] = high
            vbuf[z, c // 2, place, NX:2 * NX] = low

    def columns_step(i, carry):
        columns(i + 1)
        return carry

    unpack_sites(0, (1, 2, 3, 4))
    lax.fori_loop(0, 4, columns_step, 0)
    unpack_sites(1, (0, 5))

    def columns_outer(i, carry):
        columns(5 * i)
        return carry

    lax.fori_loop(0, 2, columns_outer, 0)

    def render(group, slot, which):
        weights = wrows[pl.ds(pl.multiple_of(group * 256 + which * 128, 128), 128), :]
        for z in range(NZL):
            drawn = [
                lax.dot_general(weights, vbuf[z, pair], (((1,), (1,)), ((), ())), preferred_element_type=F32)
                for pair in range(2)
            ]
            parts = [drawn[c // 2][:, (c % 2) * 128:(c % 2) * 128 + 128] for c in range(4)]
            if z == 0:
                for c in range(4):
                    acc[group, slot, c] = parts[c]
            else:
                through = 1.0 - acc[group, slot, 3]
                for c in range(4):
                    acc[group, slot, c] = acc[group, slot, c] + through * parts[c]

    partner = at(d + 1 - 2 * core, r)
    swaps = [
        remote(acc.at[group, 0], xrecv.at[group], x_sem.at[0, group], x_sem.at[1, group], partner)
        for group in range(2)
    ]
    exchange = [[], []]
    for group in range(2):
        for k in range(1, NC):
            other = lax.rem(chip + k, NC)
            exchange[group].append(
                remote(pieces.at[group, other], gathered.at[group, chip],
                       g_send_sem.at[group, k], g_recv_sem.at[group, k], at(2 * other + core, r))
            )

    def join(group):
        def step(n, carry):
            rows = pl.ds(pl.multiple_of(n * 8, 8), 8)
            front = core == 0
            mine = [acc[group, 1, c, rows, :] for c in range(4)]
            theirs = [xrecv[group, c, rows, :] for c in range(4)]
            near = [jnp.where(front, mine[c], theirs[c]) for c in range(4)]
            far = [jnp.where(front, theirs[c], mine[c]) for c in range(4)]
            through = 1.0 - near[3]
            for c in range(4):
                pieces[group, n, c] = near[c] + through * far[c]
            return carry

        lax.fori_loop(0, NC, step, 0, unroll=4)
        for copy in exchange[group]:
            copy.start()
        gathered[group, chip] = pieces[group, chip]

    render(0, 0, 1 - core)
    swaps[0].start()
    render(0, 1, core)
    render(1, 0, 1 - core)
    swaps[1].start()
    swaps[0].wait()
    join(0)
    render(1, 1, core)
    swaps[1].wait()
    join(1)

    for group in range(2):
        for copy in exchange[group]:
            copy.wait()
        final = [gathered[group, 0, c] for c in range(4)]
        for n in range(1, NC):
            through = 1.0 - final[3]
            final = [final[c] + through * gathered[group, n, c] for c in range(4)]
        for half in range(2):
            for c in range(4):
                fsend[2 * group + half, 4 * c:4 * c + 4, :] = final[c][4 * half:4 * half + 4, :]
    last = []
    for k in range(1, NR):
        other = lax.rem(r + k, NR)
        last.append(remote(fsend.at[other], frecv.at[r], f_send_sem.at[k], f_recv_sem.at[k], at(d, other)))
        last[-1].start()
    frecv[r] = fsend[r]
    for copy in last:
        copy.wait()
    for rr in range(NR):
        for c in range(4):
            image[c, :, rr * 128:(rr + 1) * 128] = frecv[rr, 4 * c:4 * c + 4, :]


def shards(populations, fluid_mask, tissue_tag, colour_table):
    dma = pltpu.SemaphoreType.DMA
    vmem = pl.BlockSpec(memory_space=pltpu.VMEM)
    anywhere = pl.BlockSpec(memory_space=pl.ANY)
    advanced, drawn = pl.pallas_call(
        kernel,
        out_shape=(
            pltpu.VMEM(populations.shape, F32),
            pltpu.VMEM((4, IMG // (ND * NR), IMG), F32),
        ),
        in_specs=[anywhere, anywhere, anywhere, vmem],
        out_specs=(vmem, vmem),
        scratch_shapes=[
            pltpu.VMEM((NZL, NYL, NX), jnp.int32),
            pltpu.VMEM((NZL, NYL, NX), jnp.int32),
            pltpu.VMEM((NQ, NZL + 2, 2, 48, 128), F32),
            pltpu.VMEM((NQ, NZL + 2, 2, 48, 128), F32),
            pltpu.VMEM((2, 2, NZL, 16, 128), F32),
            pltpu.VMEM((2, 2, NZL, 16, 128), F32),
            pltpu.VMEM((2, 4, 8, 128), F32),
            pltpu.VMEM((2, 4, 8, 128), F32),
            pltpu.VMEM((4, 4, 2, 2, 8, 128), F32),
            pltpu.VMEM((4, NZL, 48, NX), F32),
            pltpu.VMEM((2, 3, 8, NX), F32),
            pltpu.VMEM((2, 3, 8, NX), F32),
            pltpu.VMEM((128, 96), BF16),
            pltpu.VMEM((IMG, 2 * NX), BF16),
            pltpu.VMEM((NZL, 2, 256, 2 * NX), BF16),
            pltpu.VMEM((2, 2, 4, 128, 128), F32),
            pltpu.VMEM((2, 4, 128, 128), F32),
            pltpu.VMEM((2, NC, 4, 8, 128), F32),
            pltpu.VMEM((2, NC, 4, 8, 128), F32),
            pltpu.VMEM((NR, 16, 128), F32),
            pltpu.VMEM((NR, 16, 128), F32),
            dma((NZL + 2,)), dma((2, 8)), dma((2, 8)), dma((2, 2)), dma((2, 2)), dma((2, 2)),
            dma((2, NC)), dma((2, NC)), dma((NR,)), dma((NR,)),
        ],
        compiler_params=pltpu.CompilerParams(
            collective_id=0, has_side_effects=True, vmem_limit_bytes=56 * 2**20
        ),
        name="vessel",
    )(populations, fluid_mask, tissue_tag, colour_table)
    return pl.pallas_call(
        deliver,
        out_shape=(
            jax.ShapeDtypeStruct(populations.shape, F32),
            jax.ShapeDtypeStruct((4, IMG // (ND * NR), IMG), F32),
        ),
        in_specs=[vmem, vmem],
        out_specs=(anywhere, anywhere),
        scratch_shapes=[dma((NZL + 1,))],
        compiler_params=pltpu.CompilerParams(vmem_limit_bytes=2**20),
        name="deliver",
    )(advanced, drawn)


def deliver(advanced, drawn, adv, image, sem):
    copies = [pltpu.make_async_copy(advanced.at[:, z], adv.at[:, z], sem.at[z]) for z in range(NZL)]
    copies.append(pltpu.make_async_copy(drawn, image, sem.at[NZL]))
    for copy in copies:
        copy.start()
    for copy in copies:
        copy.wait()


def solution(mesh):
    placed = (
        P(None, "depth", "rows", None),
        P("depth", "rows", None),
        P("depth", "rows", None),
        P(),
    )
    return jax.shard_map(
        shards,
        mesh=mesh,
        in_specs=placed,
        out_specs=(P(None, "depth", "rows", None), P(None, ("rows", "depth"), None)),
        check_vma=False,
    )
```

time: 55.4 us -> 46.6 us (0.84)
  local copies, waits for them, and re-layouts: 5.05 us -> 0 us
  Pallas kernels: 49.6 us -> 45.8 us
    unnamed x4 -> x0, local copies, waits for them, and re-layouts: 5.05 us -> none
    pallas_call x1 -> x2, Pallas kernels: 49.6 us -> 45.8 us  [the longest x1 43.9 us: shards(): pl.pallas_call(kernel, out_shape=(pltpu.VMEM(populations.shape, F32), plt...]
where the time goes in v1:
time: 46.6 us; the launch traced here: 46.5 us
  Pallas kernels  45.8 us (98%)
  between operations  0.64 us (1%)
    pallas_call x1, Pallas kernels, shards(): pl.pallas_call(kernel, out_shape=(pltpu.VMEM(populations.shape, F32), plt...  43.9 us
    pallas_call x1, Pallas kernels, shards(): pl.pallas_call(deliver, out_shape=(jax.ShapeDtypeStruct(populations.shape...  1.92 us

profile of v1, /device:TPU:0, one launch (start us, length us, event | category | flops | bytes accessed | tf_op | source)
XLA Modules:
  0.0 46.5 jit_solution(13808308868316116912)
XLA Ops:
  0.6 43.9 %vessel.1 = (f32[19,6,32,256]{3,2,1,0:T(8,128)S(1)}, f32[4,4,512]{2,1,0:T(4,128)S(1)}) custom-call(f32[19,6,32,256]{3,2,1,0:T(8,128)} %pops.1, s32[6,32,256]{2,1,0:T(8,128)} %mask_in.1, s32[6,32,256]{2,1,0:T(8,128)} %tag_in.1, f32[4,4,256]{2,1,0:T(4,128)} %table.1), custom_call_target="tpu_custom_call" | custom-call | tf_op jit(solution)/shard_map/vessel/pallas_call | solution.py:544
  44.6 1.9 %deliver.1 = (f32[19,6,32,256]{3,2,1,0:T(8,128)}, f32[4,4,512]{2,1,0:T(4,128)}) custom-call(f32[19,6,32,256]{3,2,1,0:T(8,128)S(1)} %get-tuple-element.4.advanced, f32[4,4,512]{2,1,0:T(4,128)S(1)} %get-tuple-element.5.drawn), custom_call_target="tpu_custom_call" | custom-call | tf_op jit(solution)/shard_map/deliver/pallas_call | solution.py:582

commit v2 on v1

--- a/solution.py
+++ b/solution.py
@@ -101,7 +101,7 @@
     pops, mask_in, tag_in, table, pbuf, image,
     mask, tag, r1, r2, ysend, yrecv, csend, crecv, bins, cbuf, ssend, srecv, wcols, wrows, vbuf,
     acc, xrecv, pieces, gathered, fsend, frecv,
-    in_sem, hs_sem, hr_sem, c_send_sem, c_recv_sem, x_sem, g_send_sem, g_recv_sem, f_send_sem, f_recv_sem,
+    in_sem, ls_sem, lr_sem, hs_sem, hr_sem, c_send_sem, c_recv_sem, x_sem, g_send_sem, g_recv_sem, f_send_sem, f_recv_sem,
 ):
     d = lax.axis_index("depth")
     r = lax.axis_index("rows")
@@ -114,10 +114,11 @@
         return {"depth": dd, "rows": rr}
 
     barrier = pltpu.get_barrier_semaphore()
-    peers = [at(up_d, r), at(down_d, r), at(up_d, up_r), at(up_d, down_r), at(down_d, up_r), at(down_d, down_r)]
-    peers += [at(d, lax.rem(r + k, NR)) for k in range(1, NR)]
-    peers += [at(lax.rem(d + 2 * k, ND), r) for k in range(1, NC)]
-    peers += [at(d + 1 - 2 * core, r)]
+    chips = sorted(range(1, NC), key=lambda k: -min(k // 4, 4 - k // 4) - min(k % 4, 4 - k % 4))
+    peers = [at(lax.rem(d + 2 * k, ND), r) for k in chips]
+    peers += [at(up_d, up_r), at(up_d, down_r), at(down_d, up_r), at(down_d, down_r)]
+    peers += [at(d, lax.rem(r + k, NR)) for k in (2, 1, 3)]
+    peers += [at(up_d, r), at(down_d, r), at(d + 1 - 2 * core, r)]
     for peer in peers:
         pl.semaphore_signal(barrier, inc=1, device_id=peer, device_id_type=MESH)
 
@@ -148,19 +149,18 @@
             wt = jnp.maximum(0.0, 1.0 - jnp.abs(centre - xx)).astype(BF16)
             rows = pl.ds(pl.multiple_of(b * 64, 64), 64)
             wrows[rows, h * 128:(h + 1) * 128] = wt
-            wrows[rows, 256 + h * 128:256 + (h + 1) * 128] = wt
         return carry
 
     lax.fori_loop(0, IMG // 64, fill_rows, 0)
 
+    low_lanes = lane < 64
     for k in range(4):
         for c in range(4):
-            now = [jnp.broadcast_to(table[k, c:c + 1, h * 128:(h + 1) * 128], (8, 128)) for h in range(2)]
-            turned = [pltpu.roll(half, 127, 1) for half in now]
-            following = (jnp.where(last_lane, turned[1], turned[0]), jnp.where(last_lane, now[1], turned[1]))
-            for h in range(2):
-                bins[k, c, 0, h] = now[h]
-                bins[k, c, 1, h] = following[h]
+            halves = [jnp.broadcast_to(table[k, c:c + 1, h * 128:(h + 1) * 128], (8, 128)) for h in range(2)]
+            for parity in range(2):
+                index = ((lane * 2) & 127) + parity
+                taken = [jnp.take_along_axis(half, index, axis=1, mode="promise_in_bounds") for half in halves]
+                bins[k, c, parity] = jnp.where(low_lanes, taken[0], taken[1])
 
     def clear(z, carry):
         for c in range(4):
@@ -217,12 +217,10 @@
         for h in range(2):
             store_relaxed(r2, z, t, h, collide(f[h], fluids[h], WALL_REST[1]))
 
-    def lookup(c, after, low, upper, tags):
-        picked = []
-        for k in range(4):
-            a = jnp.take_along_axis(bins[k, c, after, 0], low, axis=1, mode="promise_in_bounds")
-            b = jnp.take_along_axis(bins[k, c, after, 1], low, axis=1, mode="promise_in_bounds")
-            picked.append(jnp.where(upper, b, a))
+    def lookup(c, parity, index, tags):
+        picked = [
+            jnp.take_along_axis(bins[k, c, parity], index, axis=1, mode="promise_in_bounds") for k in range(4)
+        ]
         return jnp.where(
             tags[0], jnp.where(tags[1], picked[3], picked[2]), jnp.where(tags[1], picked[1], picked[0])
         )
@@ -237,14 +235,14 @@
             tags = (tags >= 2, (tags & 1) == 1)
             place = []
             for where in places[2 * h:2 * h + 2]:
-                bin_number = jnp.clip(where.astype(jnp.int32), 0, 255)
-                place.append((where - bin_number.astype(F32), bin_number & 127, bin_number >= 128))
+                lower = jnp.clip(where.astype(jnp.int32), 0, 254)
+                even, odd = (lower + 1) >> 1, lower >> 1
+                place.append((1.0 - jnp.abs(where - (even + even).astype(F32)), even, odd))
             result = []
-            for c in range(4):
-                share, low, upper = place[1 if c == 3 else 0]
-                here = lookup(c, 0, low, upper, tags)
-                after = lookup(c, 1, low, upper, tags)
-                result.append(here + share * (after - here))
+            for (share, even, odd), channels in zip(place, ((0, 1, 2), (3,))):
+                at_odd = [lookup(c, 1, odd, tags) for c in channels]
+                at_even = [lookup(c, 0, even, tags) for c in channels]
+                result += [a + share * (b - a) for a, b in zip(at_odd, at_even)]
             coverage = jnp.where(fluids[h], result[3] * (3.0 / (NZL * ND)), 0.0)
             for c in range(3):
                 cbuf[c, z, padded, lanes] = result[c] * coverage
@@ -268,29 +266,45 @@
             body(z_of(i), t_of(i))
             return carry
 
-        lax.fori_loop(0, count, step, 0)
+        lax.fori_loop(0, count, step, 0, unroll=4)
+
+    def outer_tiles(body, after):
+        def step(t, carry):
+            body(5, t)
+            body(0, t)
+            if after is not None:
+                @pl.when(t > 0)
+                def _():
+                    for copy in after(t - 1):
+                        copy.start()
+            return carry
+
+        lax.fori_loop(0, 4, step, 0, unroll=2)
 
     def remote(src, dst, send, recv, target):
         return pltpu.make_async_remote_copy(
             src_ref=src, dst_ref=dst, send_sem=send, recv_sem=recv, device_id=target, device_id_type=MESH
         )
 
+    def layer_copies(s, rel, t):
+        rows = pl.ds(pl.multiple_of(8 * t + 8, 8), 8)
+        return [
+            remote(rel.at[UP_Z:UP_Z + 5, 6, :, rows, :], rel.at[UP_Z:UP_Z + 5, 0, :, rows, :],
+                   ls_sem.at[s, 0, t], lr_sem.at[s, 0, t], at(up_d, r)),
+            remote(rel.at[DOWN_Z:DOWN_Z + 5, 1, :, rows, :], rel.at[DOWN_Z:DOWN_Z + 5, 7, :, rows, :],
+                   ls_sem.at[s, 1, t], lr_sem.at[s, 1, t], at(down_d, r)),
+        ]
+
     def halo_copies(s, rel):
-        layers = [
-            remote(rel.at[UP_Z:UP_Z + 5, 6, :, 8:40, :], rel.at[UP_Z:UP_Z + 5, 0, :, 8:40, :],
-                   hs_sem.at[s, 0], hr_sem.at[s, 0], at(up_d, r)),
-            remote(rel.at[DOWN_Z:DOWN_Z + 5, 1, :, 8:40, :], rel.at[DOWN_Z:DOWN_Z + 5, 7, :, 8:40, :],
-                   hs_sem.at[s, 1], hr_sem.at[s, 1], at(down_d, r)),
-        ]
         rows = [
-            remote(ysend.at[s, 0], yrecv.at[s, 0], hs_sem.at[s, 2], hr_sem.at[s, 2], at(d, up_r)),
-            remote(ysend.at[s, 1], yrecv.at[s, 1], hs_sem.at[s, 3], hr_sem.at[s, 3], at(d, down_r)),
+            remote(ysend.at[s, 0], yrecv.at[s, 0], hs_sem.at[s, 0], hr_sem.at[s, 0], at(d, up_r)),
+            remote(ysend.at[s, 1], yrecv.at[s, 1], hs_sem.at[s, 1], hr_sem.at[s, 1], at(d, down_r)),
         ]
         corners = [
-            remote(csend.at[s, n], crecv.at[s, n], hs_sem.at[s, 4 + n], hr_sem.at[s, 4 + n], at(dd, rr))
+            remote(csend.at[s, n], crecv.at[s, n], hs_sem.at[s, 2 + n], hr_sem.at[s, 2 + n], at(dd, rr))
             for n, (dd, rr) in enumerate(((up_d, up_r), (down_d, down_r), (down_d, up_r), (up_d, down_r)))
         ]
-        return layers, rows, corners
+        return rows, corners
 
     corner_places = ((15, 6, 39, 0, 7), (16, 1, 8, 7, 40), (17, 1, 39, 7, 7), (18, 6, 8, 0, 40))
 
@@ -300,26 +314,22 @@
                 csend[s, n, h:h + 1, :] = rel[POS[q], layer, h, row:row + 1, :]
 
     def pack_rows(s, rel):
-        def step(z, carry):
-            for side, (slots, row) in enumerate(((UP_Y, 39), (DOWN_Y, 8))):
+        for side, (slots, row) in enumerate(((UP_Y, 39), (DOWN_Y, 8))):
+            for z in range(NZL):
                 for n, slot in enumerate(slots):
                     for h in range(2):
-                        ysend[s, side, z, 2 * n + h:2 * n + h + 1, :] = rel[slot, z + 1, h, row:row + 1, :]
-            return carry
-
-        lax.fori_loop(0, NZL, step, 0)
+                        place = 10 * z + 2 * n + h
+                        ysend[s, side, place:place + 1, :] = rel[slot, z + 1, h, row:row + 1, :]
 
     def unpack_rows(s, rel):
-        def step(z, carry):
-            for side, (slots, row, edge) in enumerate(((UP_Y, 7, r == 0), (DOWN_Y, 40, r == NR - 1))):
+        for side, (slots, row, edge) in enumerate(((UP_Y, 7, r == 0), (DOWN_Y, 40, r == NR - 1))):
+            for z in range(NZL):
                 for n, slot in enumerate(slots):
                     for h in range(2):
+                        place = 10 * z + 2 * n + h
                         rel[slot, z + 1, h, row:row + 1, :] = jnp.where(
-                            edge, WALL, yrecv[s, side, z, 2 * n + h:2 * n + h + 1, :]
+                            edge, WALL, yrecv[s, side, place:place + 1, :]
                         )
-            return carry
-
-        lax.fori_loop(0, NZL, step, 0)
 
     def unpack_layers(s, rel):
         @pl.when(d == 0)
@@ -340,18 +350,20 @@
     loads[NZL].wait()
     loads[0].wait()
     loads[5].wait()
-    tiles(8, first_tile, lambda i: (i >> 2) * 5, lambda i: i & 3)
+    outer_tiles(first_tile, None)
     pack_corners(0, r1)
     pl.semaphore_wait(barrier, len(peers))
-    layers1, rows1, corners1 = halo_copies(0, r1)
+    layers1 = [copy for t in range(4) for copy in layer_copies(0, r1, t)]
+    rows1, corners1 = halo_copies(0, r1)
     for copy in layers1 + corners1:
         copy.start()
     for z in range(1, 5):
         loads[z].wait()
-    tiles(16, first_tile, lambda i: 1 + (i >> 2), lambda i: i & 3)
+    tiles(8, first_tile, lambda i: 1 + (i >> 1), lambda i: 3 * (i & 1))
     pack_rows(0, r1)
     for copy in rows1:
         copy.start()
+    tiles(8, first_tile, lambda i: 1 + (i >> 1), lambda i: 1 + (i & 1))
 
     tiles(8, second_tile, lambda i: 1 + (i >> 1), lambda i: 1 + (i & 1))
     for copy in rows1:
@@ -361,10 +373,11 @@
     for copy in layers1 + corners1:
         copy.wait()
     unpack_layers(0, r1)
-    tiles(8, second_tile, lambda i: (i >> 2) * 5, lambda i: i & 3)
-    layers2, rows2, corners2 = halo_copies(1, r2)
+    outer_tiles(second_tile, lambda t: layer_copies(1, r2, t))
+    layers2 = [copy for t in range(4) for copy in layer_copies(1, r2, t)]
+    rows2, corners2 = halo_copies(1, r2)
     pack_corners(1, r2)
-    for copy in layers2 + corners2:
+    for copy in layers2[6:] + corners2:
         copy.start()
     pack_rows(1, r2)
     for copy in rows2:
@@ -376,10 +389,11 @@
         def step(i, places):
             last = jnp.maximum(i - 1, 0)
             first = i == 0
+            following = third_tile(z_of(i), t_of(i))
             classify(
                 jnp.where(first, before[0], z_of(last)), jnp.where(first, before[1], t_of(last)), places
             )
-            return third_tile(z_of(i), t_of(i))
+            return following
 
         return lax.fori_loop(0, count, step, carry)
 
@@ -390,17 +404,6 @@
         ]
         for part in range(2)
     ]
-    places = tuple(jnp.zeros((8, 128), F32) for _ in range(4))
-    places = third_tiles(8, lambda i: 1 + (i >> 1), lambda i: 1 + (i & 1), (1, 1), places)
-    for copy in rows2:
-        copy.wait()
-    unpack_rows(1, r2)
-    places = third_tiles(8, lambda i: 1 + (i >> 1), lambda i: 3 * (i & 1), (4, 2), places)
-    for copy in layers2 + corners2:
-        copy.wait()
-    unpack_layers(1, r2)
-    places = third_tiles(4, lambda i: (i >> 1) * 5, lambda i: 3 * (i & 1), (4, 3), places)
-
     def pack_sites(part, layers):
         for n, z in enumerate(layers):
             for side, row in enumerate((39, 8)):
@@ -421,9 +424,22 @@
                         edge, 0.0, srecv[side, 2 * part + n // 2, place:place + 1, :]
                     )
 
+    places = tuple(jnp.zeros((8, 128), F32) for _ in range(4))
+    places = third_tiles(8, lambda i: 1 + (i >> 1), lambda i: 1 + (i & 1), (1, 1), places)
+    for copy in rows2:
+        copy.wait()
+    unpack_rows(1, r2)
+    places = third_tiles(8, lambda i: 1 + (i >> 1), lambda i: 3 * (i & 1), (4, 2), places)
+    classify(4, 3, places)
     pack_sites(0, (1, 2, 3, 4))
+    for copy in layers2 + corners2:
+        copy.wait()
+    unpack_layers(1, r2)
+    places = third_tiles(4, lambda i: (i >> 1) * 5, lambda i: 3 * (i & 1), (4, 3), places)
+
+    classify(5, 3, places)
+    pack_sites(1, (0, 5))
     places = third_tiles(4, lambda i: (i >> 1) * 5, lambda i: 1 + (i & 1), (5, 3), places)
-    pack_sites(1, (0, 5))
     classify(5, 2, places)
 
     def columns(z):
@@ -438,42 +454,54 @@
             high = wide.astype(BF16)
             low = (wide - high.astype(F32)).astype(BF16)
             place = slice((c % 2) * 128, (c % 2) * 128 + 128)
-            vbuf[z, c // 2, place, 0:NX] = high
-            vbuf[z, c // 2, place, NX:2 * NX] = low
+            vbuf[z, c // 2, 0, place, :] = high
+            vbuf[z, c // 2, 1, place, :] = low
 
     def columns_step(i, carry):
         columns(i + 1)
         return carry
 
-    unpack_sites(0, (1, 2, 3, 4))
-    lax.fori_loop(0, 4, columns_step, 0)
-    unpack_sites(1, (0, 5))
+    def render(group, layers):
+        weights = wrows[group * 256:(group + 1) * 256, :]
+        for z in layers:
+            drawn = []
+            for pair in (1, 0):
+                parts = [
+                    lax.dot_general(
+                        weights, vbuf[z, pair, n], (((1,), (1,)), ((), ())), preferred_element_type=F32
+                    )
+                    for n in range(2)
+                ]
+                drawn.append(parts[0] + parts[1])
+            for half in range(2):
+                rows = slice(half * 128, half * 128 + 128)
+                parts = [drawn[1 - c // 2][rows, (c % 2) * 128:(c % 2) * 128 + 128] for c in range(4)]
+                if z == 0:
+                    through = 1.0 - parts[3]
+                    parts = [parts[c] + through * acc[group, half, c] for c in range(4)]
+                elif z > 1:
+                    through = 1.0 - acc[group, half, 3]
+                    parts = [acc[group, half, c] + through * parts[c] for c in range(4)]
+                for c in range(4):
+                    acc[group, half, c] = parts[c]
+
+    def columns_inner(i, carry):
+        columns(i + 1)
+        return carry
 
     def columns_outer(i, carry):
         columns(5 * i)
         return carry
 
+    unpack_sites(0, (1, 2, 3, 4))
+    lax.fori_loop(0, 4, columns_inner, 0)
+    render(0, (1, 2, 3, 4))
+    unpack_sites(1, (0, 5))
     lax.fori_loop(0, 2, columns_outer, 0)
-
-    def render(group, slot, which):
-        weights = wrows[pl.ds(pl.multiple_of(group * 256 + which * 128, 128), 128), :]
-        for z in range(NZL):
-            drawn = [
-                lax.dot_general(weights, vbuf[z, pair], (((1,), (1,)), ((), ())), preferred_element_type=F32)
-                for pair in range(2)
-            ]
-            parts = [drawn[c // 2][:, (c % 2) * 128:(c % 2) * 128 + 128] for c in range(4)]
-            if z == 0:
-                for c in range(4):
-                    acc[group, slot, c] = parts[c]
-            else:
-                through = 1.0 - acc[group, slot, 3]
-                for c in range(4):
-                    acc[group, slot, c] = acc[group, slot, c] + through * parts[c]
 
     partner = at(d + 1 - 2 * core, r)
     swaps = [
-        remote(acc.at[group, 0], xrecv.at[group], x_sem.at[0, group], x_sem.at[1, group], partner)
+        remote(acc.at[group, 1 - core], xrecv.at[group], x_sem.at[0, group], x_sem.at[1, group], partner)
         for group in range(2)
     ]
     exchange = [[], []]
@@ -489,7 +517,7 @@
         def step(n, carry):
             rows = pl.ds(pl.multiple_of(n * 8, 8), 8)
             front = core == 0
-            mine = [acc[group, 1, c, rows, :] for c in range(4)]
+            mine = [acc[group, core, c, rows, :] for c in range(4)]
             theirs = [xrecv[group, c, rows, :] for c in range(4)]
             near = [jnp.where(front, mine[c], theirs[c]) for c in range(4)]
             far = [jnp.where(front, theirs[c], mine[c]) for c in range(4)]
@@ -503,14 +531,12 @@
             copy.start()
         gathered[group, chip] = pieces[group, chip]
 
-    render(0, 0, 1 - core)
+    render(0, (0, 5))
     swaps[0].start()
-    render(0, 1, core)
-    render(1, 0, 1 - core)
+    render(1, (1, 2, 3, 4, 0, 5))
     swaps[1].start()
     swaps[0].wait()
     join(0)
-    render(1, 1, core)
     swaps[1].wait()
     join(1)
 
@@ -554,24 +580,24 @@
             pltpu.VMEM((NZL, NYL, NX), jnp.int32),
             pltpu.VMEM((NQ, NZL + 2, 2, 48, 128), F32),
             pltpu.VMEM((NQ, NZL + 2, 2, 48, 128), F32),
-            pltpu.VMEM((2, 2, NZL, 16, 128), F32),
-            pltpu.VMEM((2, 2, NZL, 16, 128), F32),
+            pltpu.VMEM((2, 2, 64, 128), F32),
+            pltpu.VMEM((2, 2, 64, 128), F32),
             pltpu.VMEM((2, 4, 8, 128), F32),
             pltpu.VMEM((2, 4, 8, 128), F32),
-            pltpu.VMEM((4, 4, 2, 2, 8, 128), F32),
+            pltpu.VMEM((4, 4, 2, 8, 128), F32),
             pltpu.VMEM((4, NZL, 48, NX), F32),
             pltpu.VMEM((2, 3, 8, NX), F32),
             pltpu.VMEM((2, 3, 8, NX), F32),
             pltpu.VMEM((128, 96), BF16),
-            pltpu.VMEM((IMG, 2 * NX), BF16),
-            pltpu.VMEM((NZL, 2, 256, 2 * NX), BF16),
+            pltpu.VMEM((IMG, NX), BF16),
+            pltpu.VMEM((NZL, 2, 2, 256, NX), BF16),
             pltpu.VMEM((2, 2, 4, 128, 128), F32),
             pltpu.VMEM((2, 4, 128, 128), F32),
             pltpu.VMEM((2, NC, 4, 8, 128), F32),
             pltpu.VMEM((2, NC, 4, 8, 128), F32),
             pltpu.VMEM((NR, 16, 128), F32),
             pltpu.VMEM((NR, 16, 128), F32),
-            dma((NZL + 2,)), dma((2, 8)), dma((2, 8)), dma((2, 2)), dma((2, 2)), dma((2, 2)),
+            dma((NZL + 2,)), dma((2, 2, 4)), dma((2, 2, 4)), dma((2, 6)), dma((2, 6)), dma((2, 2)), dma((2, 2)), dma((2, 2)),
             dma((2, NC)), dma((2, NC)), dma((NR,)), dma((NR,)),
         ],
         compiler_params=pltpu.CompilerParams(

time: 46.6 us -> 43 us (0.923)
  Pallas kernels: 45.8 us -> 42.2 us
    pallas_call x1, Pallas kernels: 43.9 us -> 40.3 us  [shards(): pl.pallas_call(kernel, out_shape=(pltpu.VMEM(populations.shape, F32), plt...]
where the time goes in v2:
time: 43 us; the launch traced here: 42.8 us
  Pallas kernels  42.2 us (98%)
  between operations  0.64 us (1%)
    pallas_call x1, Pallas kernels, shards(): pl.pallas_call(kernel, out_shape=(pltpu.VMEM(populations.shape, F32), plt...  40.3 us
    pallas_call x1, Pallas kernels, shards(): pl.pallas_call(deliver, out_shape=(jax.ShapeDtypeStruct(populations.shape...  1.92 us

profile of v2, /device:TPU:0, one launch (start us, length us, event | category | flops | bytes accessed | tf_op | source)
XLA Modules:
  0.0 42.8 jit_solution(14842487763539409364)
XLA Ops:
  0.6 40.3 %vessel.1 = (f32[19,6,32,256]{3,2,1,0:T(8,128)S(1)}, f32[4,4,512]{2,1,0:T(4,128)S(1)}) custom-call(f32[19,6,32,256]{3,2,1,0:T(8,128)} %pops.1, s32[6,32,256]{2,1,0:T(8,128)} %mask_in.1, s32[6,32,256]{2,1,0:T(8,128)} %tag_in.1, f32[4,4,256]{2,1,0:T(4,128)} %table.1), custom_call_target="tpu_custom_call" | custom-call | tf_op jit(solution)/shard_map/vessel/pallas_call | solution.py:570
  40.9 1.9 %deliver.1 = (f32[19,6,32,256]{3,2,1,0:T(8,128)}, f32[4,4,512]{2,1,0:T(4,128)}) custom-call(f32[19,6,32,256]{3,2,1,0:T(8,128)S(1)} %get-tuple-element.4.advanced, f32[4,4,512]{2,1,0:T(4,128)S(1)} %get-tuple-element.5.drawn), custom_call_target="tpu_custom_call" | custom-call | tf_op jit(solution)/shard_map/deliver/pallas_call | solution.py:608

commit v3 on v2

--- a/solution.py
+++ b/solution.py
@@ -101,7 +101,7 @@
     pops, mask_in, tag_in, table, pbuf, image,
     mask, tag, r1, r2, ysend, yrecv, csend, crecv, bins, cbuf, ssend, srecv, wcols, wrows, vbuf,
     acc, xrecv, pieces, gathered, fsend, frecv,
-    in_sem, ls_sem, lr_sem, hs_sem, hr_sem, c_send_sem, c_recv_sem, x_sem, g_send_sem, g_recv_sem, f_send_sem, f_recv_sem,
+    in_sem, ls_sem, lr_sem, hs_sem, hr_sem, c_send_sem, c_recv_sem, x_sem, g_send_sem, g_recv_sem, f_send_sem, f_recv_sem, ready,
 ):
     d = lax.axis_index("depth")
     r = lax.axis_index("rows")
@@ -114,11 +114,13 @@
         return {"depth": dd, "rows": rr}
 
     barrier = pltpu.get_barrier_semaphore()
-    chips = sorted(range(1, NC), key=lambda k: -min(k // 4, 4 - k // 4) - min(k % 4, 4 - k % 4))
-    peers = [at(lax.rem(d + 2 * k, ND), r) for k in chips]
-    peers += [at(up_d, up_r), at(up_d, down_r), at(down_d, up_r), at(down_d, down_r)]
-    peers += [at(d, lax.rem(r + k, NR)) for k in (2, 1, 3)]
-    peers += [at(up_d, r), at(down_d, r), at(d + 1 - 2 * core, r)]
+    row_first = (chip // 4) * 4
+    columns_peers = [at(2 * lax.rem(chip + 4 * k, NC) + core, r) for k in (2, 1, 3)]
+    peers = [at(up_d, up_r), at(up_d, down_r), at(down_d, up_r), at(down_d, down_r)]
+    peers += [at(d, lax.rem(r + 2, NR))]
+    peers += columns_peers
+    peers += [at(2 * (row_first + lax.rem(chip + k, 4)) + core, r) for k in (2, 1, 3)]
+    peers += [at(up_d, r), at(down_d, r), at(d, up_r), at(d, down_r), at(d + 1 - 2 * core, r)]
     for peer in peers:
         pl.semaphore_signal(barrier, inc=1, device_id=peer, device_id_type=MESH)
 
@@ -297,11 +299,15 @@
 
     def halo_copies(s, rel):
         rows = [
-            remote(ysend.at[s, 0], yrecv.at[s, 0], hs_sem.at[s, 0], hr_sem.at[s, 0], at(d, up_r)),
-            remote(ysend.at[s, 1], yrecv.at[s, 1], hs_sem.at[s, 1], hr_sem.at[s, 1], at(d, down_r)),
+            [
+                remote(ysend.at[s, side, part], yrecv.at[s, side, part], hs_sem.at[s, 4 * n + side],
+                       hr_sem.at[s, 4 * n + side], target)
+                for side, target in enumerate((at(d, up_r), at(d, down_r)))
+            ]
+            for n, part in enumerate((slice(0, 40), slice(40, 64)))
         ]
         corners = [
-            remote(csend.at[s, n], crecv.at[s, n], hs_sem.at[s, 2 + n], hr_sem.at[s, 2 + n], at(dd, rr))
+            remote(csend.at[s, n], crecv.at[s, n], hs_sem.at[s, 8 + n], hr_sem.at[s, 8 + n], at(dd, rr))
             for n, (dd, rr) in enumerate(((up_d, up_r), (down_d, down_r), (down_d, up_r), (up_d, down_r)))
         ]
         return rows, corners
@@ -313,23 +319,21 @@
             for h in range(2):
                 csend[s, n, h:h + 1, :] = rel[POS[q], layer, h, row:row + 1, :]
 
-    def pack_rows(s, rel):
+    row_places = [[(10 * n + k, z, k // 2, k % 2) for n, z in enumerate(layers) for k in range(10)] for layers in (
+        (1, 2, 3, 4), (None, None, None, None, 0, 5))]
+    row_places = [[p for p in places if p[1] is not None] for places in row_places]
+
+    def pack_rows(s, rel, part):
         for side, (slots, row) in enumerate(((UP_Y, 39), (DOWN_Y, 8))):
-            for z in range(NZL):
-                for n, slot in enumerate(slots):
-                    for h in range(2):
-                        place = 10 * z + 2 * n + h
-                        ysend[s, side, place:place + 1, :] = rel[slot, z + 1, h, row:row + 1, :]
-
-    def unpack_rows(s, rel):
+            for place, z, n, h in row_places[part]:
+                ysend[s, side, place:place + 1, :] = rel[slots[n], z + 1, h, row:row + 1, :]
+
+    def unpack_rows(s, rel, part):
         for side, (slots, row, edge) in enumerate(((UP_Y, 7, r == 0), (DOWN_Y, 40, r == NR - 1))):
-            for z in range(NZL):
-                for n, slot in enumerate(slots):
-                    for h in range(2):
-                        place = 10 * z + 2 * n + h
-                        rel[slot, z + 1, h, row:row + 1, :] = jnp.where(
-                            edge, WALL, yrecv[s, side, place:place + 1, :]
-                        )
+            for place, z, n, h in row_places[part]:
+                rel[slots[n], z + 1, h, row:row + 1, :] = jnp.where(
+                    edge, WALL, yrecv[s, side, place:place + 1, :]
+                )
 
     def unpack_layers(s, rel):
         @pl.when(d == 0)
@@ -357,30 +361,37 @@
     rows1, corners1 = halo_copies(0, r1)
     for copy in layers1 + corners1:
         copy.start()
+    for peer in columns_peers:
+        pl.semaphore_signal(ready, inc=1, device_id=peer, device_id_type=MESH)
+    pack_rows(0, r1, 1)
+    for copy in rows1[1]:
+        copy.start()
     for z in range(1, 5):
         loads[z].wait()
     tiles(8, first_tile, lambda i: 1 + (i >> 1), lambda i: 3 * (i & 1))
-    pack_rows(0, r1)
-    for copy in rows1:
+    pack_rows(0, r1, 0)
+    for copy in rows1[0]:
         copy.start()
     tiles(8, first_tile, lambda i: 1 + (i >> 1), lambda i: 1 + (i & 1))
 
     tiles(8, second_tile, lambda i: 1 + (i >> 1), lambda i: 1 + (i & 1))
-    for copy in rows1:
-        copy.wait()
-    unpack_rows(0, r1)
+    for part in (1, 0):
+        for copy in rows1[part]:
+            copy.wait()
+        unpack_rows(0, r1, part)
     tiles(8, second_tile, lambda i: 1 + (i >> 1), lambda i: 3 * (i & 1))
     for copy in layers1 + corners1:
         copy.wait()
     unpack_layers(0, r1)
+    rows2, corners2 = halo_copies(1, r2)
+    pack_rows(1, r2, 0)
+    for copy in rows2[0]:
+        copy.start()
     outer_tiles(second_tile, lambda t: layer_copies(1, r2, t))
     layers2 = [copy for t in range(4) for copy in layer_copies(1, r2, t)]
-    rows2, corners2 = halo_copies(1, r2)
+    pack_rows(1, r2, 1)
     pack_corners(1, r2)
-    for copy in layers2[6:] + corners2:
-        copy.start()
-    pack_rows(1, r2)
-    for copy in rows2:
+    for copy in rows2[1] + layers2[6:] + corners2:
         copy.start()
 
     loads[NZL + 1].wait()
@@ -426,10 +437,14 @@
 
     places = tuple(jnp.zeros((8, 128), F32) for _ in range(4))
     places = third_tiles(8, lambda i: 1 + (i >> 1), lambda i: 1 + (i & 1), (1, 1), places)
-    for copy in rows2:
+    for copy in rows2[0]:
         copy.wait()
-    unpack_rows(1, r2)
-    places = third_tiles(8, lambda i: 1 + (i >> 1), lambda i: 3 * (i & 1), (4, 2), places)
+    unpack_rows(1, r2, 0)
+    places = third_tiles(4, lambda i: 2 + (i >> 1), lambda i: 3 * (i & 1), (4, 2), places)
+    for copy in rows2[1]:
+        copy.wait()
+    unpack_rows(1, r2, 1)
+    places = third_tiles(4, lambda i: 1 + 3 * (i >> 1), lambda i: 3 * (i & 1), (3, 3), places)
     classify(4, 3, places)
     pack_sites(0, (1, 2, 3, 4))
     for copy in layers2 + corners2:
@@ -527,6 +542,8 @@
             return carry
 
         lax.fori_loop(0, NC, step, 0, unroll=4)
+        if group == 0:
+            pl.semaphore_wait(ready, len(columns_peers))
         for copy in exchange[group]:
             copy.start()
         gathered[group, chip] = pieces[group, chip]
@@ -597,8 +614,8 @@
             pltpu.VMEM((2, NC, 4, 8, 128), F32),
             pltpu.VMEM((NR, 16, 128), F32),
             pltpu.VMEM((NR, 16, 128), F32),
-            dma((NZL + 2,)), dma((2, 2, 4)), dma((2, 2, 4)), dma((2, 6)), dma((2, 6)), dma((2, 2)), dma((2, 2)), dma((2, 2)),
-            dma((2, NC)), dma((2, NC)), dma((NR,)), dma((NR,)),
+            dma((NZL + 2,)), dma((2, 2, 4)), dma((2, 2, 4)), dma((2, 12)), dma((2, 12)), dma((2, 2)), dma((2, 2)), dma((2, 2)),
+            dma((2, NC)), dma((2, NC)), dma((NR,)), dma((NR,)), pltpu.SemaphoreType.REGULAR,
         ],
         compiler_params=pltpu.CompilerParams(
             collective_id=0, has_side_effects=True, vmem_limit_bytes=56 * 2**20

time: 43 us -> 41.5 us (0.965)
  Pallas kernels: 42.2 us -> 40.7 us
    pallas_call x1, Pallas kernels: 40.3 us -> 38.8 us  [shards(): pl.pallas_call(kernel, out_shape=(pltpu.VMEM(populations.shape, F32), plt...]
where the time goes in v3:
time: 41.5 us; the launch traced here: 41.3 us
  Pallas kernels  40.7 us (98%)
  between operations  0.64 us (2%)
    pallas_call x1, Pallas kernels, shards(): pl.pallas_call(kernel, out_shape=(pltpu.VMEM(populations.shape, F32), plt...  38.8 us
    pallas_call x1, Pallas kernels, shards(): pl.pallas_call(deliver, out_shape=(jax.ShapeDtypeStruct(populations.shape...  1.92 us

profile of v3, /device:TPU:0, one launch (start us, length us, event | category | flops | bytes accessed | tf_op | source)
XLA Modules:
  0.0 41.3 jit_solution(3722663966566989997)
XLA Ops:
  0.6 38.8 %vessel.1 = (f32[19,6,32,256]{3,2,1,0:T(8,128)S(1)}, f32[4,4,512]{2,1,0:T(4,128)S(1)}) custom-call(f32[19,6,32,256]{3,2,1,0:T(8,128)} %pops.1, s32[6,32,256]{2,1,0:T(8,128)} %mask_in.1, s32[6,32,256]{2,1,0:T(8,128)} %tag_in.1, f32[4,4,256]{2,1,0:T(4,128)} %table.1), custom_call_target="tpu_custom_call" | custom-call | tf_op jit(solution)/shard_map/vessel/pallas_call | solution.py:587
  39.4 1.9 %deliver.1 = (f32[19,6,32,256]{3,2,1,0:T(8,128)}, f32[4,4,512]{2,1,0:T(4,128)}) custom-call(f32[19,6,32,256]{3,2,1,0:T(8,128)S(1)} %get-tuple-element.4.advanced, f32[4,4,512]{2,1,0:T(4,128)S(1)} %get-tuple-element.5.drawn), custom_call_target="tpu_custom_call" | custom-call | tf_op jit(solution)/shard_map/deliver/pallas_call | solution.py:625

commit v4 on v3

--- a/solution.py
+++ b/solution.py
@@ -164,6 +164,15 @@
                 taken = [jnp.take_along_axis(half, index, axis=1, mode="promise_in_bounds") for half in halves]
                 bins[k, c, parity] = jnp.where(low_lanes, taken[0], taken[1])
 
+    for rel in (r1, r2):
+        @pl.when(d == 0)
+        def _():
+            rel[UP_Z:UP_Z + 5, 0, :, 8:40, :] = jnp.full((5, 2, 32, 128), WALL, F32)
+
+        @pl.when(d == ND - 1)
+        def _():
+            rel[DOWN_Z:DOWN_Z + 5, 7, :, 8:40, :] = jnp.full((5, 2, 32, 128), WALL, F32)
+
     def clear(z, carry):
         for c in range(4):
             cbuf[c, z, 0:8, :] = jnp.zeros((8, NX), F32)
@@ -270,45 +279,61 @@
 
         lax.fori_loop(0, count, step, 0, unroll=4)
 
-    def outer_tiles(body, after):
-        def step(t, carry):
+    def outer_tiles(body, before, after):
+        for t in range(4):
+            if before is not None:
+                before(t)
             body(5, t)
             body(0, t)
-            if after is not None:
-                @pl.when(t > 0)
-                def _():
-                    for copy in after(t - 1):
-                        copy.start()
-            return carry
-
-        lax.fori_loop(0, 4, step, 0, unroll=2)
+            if after is not None and t:
+                start(after[2 * t - 2:2 * t])
 
     def remote(src, dst, send, recv, target):
         return pltpu.make_async_remote_copy(
             src_ref=src, dst_ref=dst, send_sem=send, recv_sem=recv, device_id=target, device_id_type=MESH
         )
 
+    to_up, to_down, from_down, from_up = d < ND - 1, d > 0, d > 0, d < ND - 1
+    to_right, to_left, from_left, from_right = r < NR - 1, r > 0, r > 0, r < NR - 1
+
+    def start(copies):
+        for copy, sends, _ in copies:
+            pl.when(sends)(copy.start)
+
+    def finish(copies):
+        for copy, sends, receives in copies:
+            pl.when(receives)(copy.wait_recv)
+            pl.when(sends)(copy.wait_send)
+
     def layer_copies(s, rel, t):
-        rows = pl.ds(pl.multiple_of(8 * t + 8, 8), 8)
+        rows = pl.ds(8 * t + 8, 8)
         return [
-            remote(rel.at[UP_Z:UP_Z + 5, 6, :, rows, :], rel.at[UP_Z:UP_Z + 5, 0, :, rows, :],
-                   ls_sem.at[s, 0, t], lr_sem.at[s, 0, t], at(up_d, r)),
-            remote(rel.at[DOWN_Z:DOWN_Z + 5, 1, :, rows, :], rel.at[DOWN_Z:DOWN_Z + 5, 7, :, rows, :],
-                   ls_sem.at[s, 1, t], lr_sem.at[s, 1, t], at(down_d, r)),
+            (remote(rel.at[UP_Z:UP_Z + 5, 6, :, rows, :], rel.at[UP_Z:UP_Z + 5, 0, :, rows, :],
+                    ls_sem.at[s, 0, t], lr_sem.at[s, 0, t], at(up_d, r)), to_up, from_down),
+            (remote(rel.at[DOWN_Z:DOWN_Z + 5, 1, :, rows, :], rel.at[DOWN_Z:DOWN_Z + 5, 7, :, rows, :],
+                    ls_sem.at[s, 1, t], lr_sem.at[s, 1, t], at(down_d, r)), to_down, from_up),
         ]
+
+    sides = ((at(d, up_r), to_right, from_left), (at(d, down_r), to_left, from_right))
+    corner_sides = (
+        (at(up_d, up_r), to_up & to_right, from_down & from_left),
+        (at(down_d, down_r), to_down & to_left, from_up & from_right),
+        (at(down_d, up_r), to_down & to_right, from_up & from_left),
+        (at(up_d, down_r), to_up & to_left, from_down & from_right),
+    )
 
     def halo_copies(s, rel):
         rows = [
             [
-                remote(ysend.at[s, side, part], yrecv.at[s, side, part], hs_sem.at[s, 4 * n + side],
-                       hr_sem.at[s, 4 * n + side], target)
-                for side, target in enumerate((at(d, up_r), at(d, down_r)))
+                (remote(ysend.at[s, side, part], yrecv.at[s, side, part], hs_sem.at[s, 4 * n + side],
+                        hr_sem.at[s, 4 * n + side], target), sends, receives)
+                for side, (target, sends, receives) in enumerate(sides)
             ]
             for n, part in enumerate((slice(0, 40), slice(40, 64)))
         ]
         corners = [
-            remote(csend.at[s, n], crecv.at[s, n], hs_sem.at[s, 8 + n], hr_sem.at[s, 8 + n], at(dd, rr))
-            for n, (dd, rr) in enumerate(((up_d, up_r), (down_d, down_r), (down_d, up_r), (up_d, down_r)))
+            (remote(csend.at[s, n], crecv.at[s, n], hs_sem.at[s, 8 + n], hr_sem.at[s, 8 + n], target), sends, receives)
+            for n, (target, sends, receives) in enumerate(corner_sides)
         ]
         return rows, corners
 
@@ -335,15 +360,11 @@
                     edge, WALL, yrecv[s, side, place:place + 1, :]
                 )
 
-    def unpack_layers(s, rel):
-        @pl.when(d == 0)
-        def _():
-            rel[UP_Z:UP_Z + 5, 0] = jnp.full((5, 2, 48, 128), WALL, F32)
-
-        @pl.when(d == ND - 1)
-        def _():
-            rel[DOWN_Z:DOWN_Z + 5, 7] = jnp.full((5, 2, 48, 128), WALL, F32)
-
+    def take_layers(copies, t):
+        finish(copies[2 * t:2 * t + 2])
+
+    def take_corners(s, copies, rel):
+        finish(copies)
         edges = (
             (d == 0) | (r == 0), (d == ND - 1) | (r == NR - 1), (d == ND - 1) | (r == 0), (d == 0) | (r == NR - 1)
         )
@@ -354,45 +375,38 @@
     loads[NZL].wait()
     loads[0].wait()
     loads[5].wait()
-    outer_tiles(first_tile, None)
+    outer_tiles(first_tile, None, None)
     pack_corners(0, r1)
     pl.semaphore_wait(barrier, len(peers))
     layers1 = [copy for t in range(4) for copy in layer_copies(0, r1, t)]
     rows1, corners1 = halo_copies(0, r1)
-    for copy in layers1 + corners1:
-        copy.start()
+    start(layers1 + corners1)
     for peer in columns_peers:
         pl.semaphore_signal(ready, inc=1, device_id=peer, device_id_type=MESH)
     pack_rows(0, r1, 1)
-    for copy in rows1[1]:
-        copy.start()
+    start(rows1[1])
     for z in range(1, 5):
         loads[z].wait()
     tiles(8, first_tile, lambda i: 1 + (i >> 1), lambda i: 3 * (i & 1))
     pack_rows(0, r1, 0)
-    for copy in rows1[0]:
-        copy.start()
+    start(rows1[0])
     tiles(8, first_tile, lambda i: 1 + (i >> 1), lambda i: 1 + (i & 1))
 
     tiles(8, second_tile, lambda i: 1 + (i >> 1), lambda i: 1 + (i & 1))
     for part in (1, 0):
-        for copy in rows1[part]:
-            copy.wait()
+        finish(rows1[part])
         unpack_rows(0, r1, part)
     tiles(8, second_tile, lambda i: 1 + (i >> 1), lambda i: 3 * (i & 1))
-    for copy in layers1 + corners1:
-        copy.wait()
-    unpack_layers(0, r1)
     rows2, corners2 = halo_copies(1, r2)
     pack_rows(1, r2, 0)
-    for copy in rows2[0]:
-        copy.start()
-    outer_tiles(second_tile, lambda t: layer_copies(1, r2, t))
+    start(rows2[0])
     layers2 = [copy for t in range(4) for copy in layer_copies(1, r2, t)]
+    take_corners(0, corners1, r1)
+    take_layers(layers1, 0)
+    outer_tiles(second_tile, lambda t: take_layers(layers1, t + 1) if t < 3 else None, layers2)
     pack_rows(1, r2, 1)
     pack_corners(1, r2)
-    for copy in rows2[1] + layers2[6:] + corners2:
-        copy.start()
+    start(layers2[6:] + rows2[1] + corners2)
 
     loads[NZL + 1].wait()
 
@@ -410,10 +424,11 @@
 
     site_copies = [
         [
-            remote(ssend.at[side, 2 * part:3 - (1 - part)], srecv.at[side, 2 * part:3 - (1 - part)], c_send_sem.at[part, side], c_recv_sem.at[part, side], target)
-            for side, target in enumerate((at(d, up_r), at(d, down_r)))
+            (remote(ssend.at[side, slots], srecv.at[side, slots], c_send_sem.at[part, side],
+                    c_recv_sem.at[part, side], target), sends, receives)
+            for side, (target, sends, receives) in enumerate(sides)
         ]
-        for part in range(2)
+        for part, slots in enumerate((slice(0, 2), slice(2, 3)))
     ]
     def pack_sites(part, layers):
         for n, z in enumerate(layers):
@@ -421,12 +436,10 @@
                 for c in range(4):
                     place = 4 * (n % 2) + c
                     ssend[side, 2 * part + n // 2, place:place + 1, :] = cbuf[c, z, row:row + 1, :]
-        for copy in site_copies[part]:
-            copy.start()
+        start(site_copies[part])
 
     def unpack_sites(part, layers):
-        for copy in site_copies[part]:
-            copy.wait()
+        finish(site_copies[part])
         for n, z in enumerate(layers):
             for side, (row, edge) in enumerate(((7, r == 0), (40, r == NR - 1))):
                 for c in range(4):
@@ -437,20 +450,21 @@
 
     places = tuple(jnp.zeros((8, 128), F32) for _ in range(4))
     places = third_tiles(8, lambda i: 1 + (i >> 1), lambda i: 1 + (i & 1), (1, 1), places)
-    for copy in rows2[0]:
-        copy.wait()
+    finish(rows2[0])
     unpack_rows(1, r2, 0)
     places = third_tiles(4, lambda i: 2 + (i >> 1), lambda i: 3 * (i & 1), (4, 2), places)
-    for copy in rows2[1]:
-        copy.wait()
+    finish(rows2[1])
     unpack_rows(1, r2, 1)
     places = third_tiles(4, lambda i: 1 + 3 * (i >> 1), lambda i: 3 * (i & 1), (3, 3), places)
     classify(4, 3, places)
     pack_sites(0, (1, 2, 3, 4))
-    for copy in layers2 + corners2:
-        copy.wait()
-    unpack_layers(1, r2)
-    places = third_tiles(4, lambda i: (i >> 1) * 5, lambda i: 3 * (i & 1), (4, 3), places)
+    take_corners(1, corners2, r2)
+    for t in range(2):
+        take_layers(layers2, t)
+    places = third_tiles(2, lambda i: i * 5, lambda i: 0, (4, 3), places)
+    for t in range(2, 4):
+        take_layers(layers2, t)
+    places = third_tiles(2, lambda i: i * 5, lambda i: 3, (5, 0), places)
 
     classify(5, 3, places)
     pack_sites(1, (0, 5))
@@ -519,9 +533,10 @@
         remote(acc.at[group, 1 - core], xrecv.at[group], x_sem.at[0, group], x_sem.at[1, group], partner)
         for group in range(2)
     ]
+    chips = list(range(1, NC))
     exchange = [[], []]
     for group in range(2):
-        for k in range(1, NC):
+        for k in chips:
             other = lax.rem(chip + k, NC)
             exchange[group].append(
                 remote(pieces.at[group, other], gathered.at[group, chip],
@@ -630,15 +645,16 @@
         ),
         in_specs=[vmem, vmem],
         out_specs=(anywhere, anywhere),
-        scratch_shapes=[dma((NZL + 1,))],
+        scratch_shapes=[dma((8,))],
         compiler_params=pltpu.CompilerParams(vmem_limit_bytes=2**20),
         name="deliver",
     )(advanced, drawn)
 
 
 def deliver(advanced, drawn, adv, image, sem):
-    copies = [pltpu.make_async_copy(advanced.at[:, z], adv.at[:, z], sem.at[z]) for z in range(NZL)]
-    copies.append(pltpu.make_async_copy(drawn, image, sem.at[NZL]))
+    parts = [slice(3 * n, min(3 * n + 3, NQ)) for n in range(7)]
+    copies = [pltpu.make_async_copy(advanced.at[p], adv.at[p], sem.at[n]) for n, p in enumerate(parts)]
+    copies.append(pltpu.make_async_copy(drawn, image, sem.at[7]))
     for copy in copies:
         copy.start()
     for copy in copies:

time: 41.5 us -> 40.3 us (0.971)
  Pallas kernels: 40.7 us -> 39.4 us
    pallas_call x1, Pallas kernels: 38.8 us -> 37.5 us  [shards(): pl.pallas_call(kernel, out_shape=(pltpu.VMEM(populations.shape, F32), plt...]
where the time goes in v4:
time: 40.3 us; the launch traced here: 40.1 us
  Pallas kernels  39.4 us (98%)
  between operations  0.64 us (2%)
    pallas_call x1, Pallas kernels, shards(): pl.pallas_call(kernel, out_shape=(pltpu.VMEM(populations.shape, F32), plt...  37.5 us
    pallas_call x1, Pallas kernels, shards(): pl.pallas_call(deliver, out_shape=(jax.ShapeDtypeStruct(populations.shape...  1.92 us

profile of v4, /device:TPU:0, one launch (start us, length us, event | category | flops | bytes accessed | tf_op | source)
XLA Modules:
  0.0 40.1 jit_solution(4636727498997942019)
XLA Ops:
  0.6 37.5 %vessel.1 = (f32[19,6,32,256]{3,2,1,0:T(8,128)S(1)}, f32[4,4,512]{2,1,0:T(4,128)S(1)}) custom-call(f32[19,6,32,256]{3,2,1,0:T(8,128)} %pops.1, s32[6,32,256]{2,1,0:T(8,128)} %mask_in.1, s32[6,32,256]{2,1,0:T(8,128)} %tag_in.1, f32[4,4,256]{2,1,0:T(4,128)} %table.1), custom_call_target="tpu_custom_call" | custom-call | tf_op jit(solution)/shard_map/vessel/pallas_call | solution.py:602
  38.2 1.9 %deliver.1 = (f32[19,6,32,256]{3,2,1,0:T(8,128)}, f32[4,4,512]{2,1,0:T(4,128)}) custom-call(f32[19,6,32,256]{3,2,1,0:T(8,128)S(1)} %get-tuple-element.4.advanced, f32[4,4,512]{2,1,0:T(4,128)S(1)} %get-tuple-element.5.drawn), custom_call_target="tpu_custom_call" | custom-call | tf_op jit(solution)/shard_map/deliver/pallas_call | solution.py:640

commit v5 on v4

--- a/solution.py
+++ b/solution.py
@@ -35,6 +35,8 @@
 WALL = -1e30
 WALL_REST = (-1e8, -1e12)
 LIMIT = -1e5
+
+RED_STEPS, GREEN_STEPS = 32767.0, 65535.0
 
 NQ, NZL, NYL, NX = 19, 6, 32, 256
 ND, NR, NC = 32, 4, 16
@@ -99,7 +101,7 @@
 
 def kernel(
     pops, mask_in, tag_in, table, pbuf, image,
-    mask, tag, r1, r2, ysend, yrecv, csend, crecv, bins, cbuf, ssend, srecv, wcols, wrows, vbuf,
+    mask, tag, r1, r2, ysend, yrecv, csend, crecv, bins, pairs, cbuf, ssend, srecv, wcols, wrows, vbuf,
     acc, xrecv, pieces, gathered, fsend, frecv,
     in_sem, ls_sem, lr_sem, hs_sem, hr_sem, c_send_sem, c_recv_sem, x_sem, g_send_sem, g_recv_sem, f_send_sem, f_recv_sem, ready,
 ):
@@ -157,12 +159,18 @@
 
     low_lanes = lane < 64
     for k in range(4):
-        for c in range(4):
-            halves = [jnp.broadcast_to(table[k, c:c + 1, h * 128:(h + 1) * 128], (8, 128)) for h in range(2)]
-            for parity in range(2):
-                index = ((lane * 2) & 127) + parity
+        for parity in range(2):
+            index = ((lane * 2) & 127) + parity
+            entries = []
+            for c in range(4):
+                halves = [jnp.broadcast_to(table[k, c:c + 1, h * 128:(h + 1) * 128], (8, 128)) for h in range(2)]
                 taken = [jnp.take_along_axis(half, index, axis=1, mode="promise_in_bounds") for half in halves]
-                bins[k, c, parity] = jnp.where(low_lanes, taken[0], taken[1])
+                entries.append(jnp.where(low_lanes, taken[0], taken[1]))
+            red = (entries[0] * RED_STEPS + 0.5).astype(jnp.int32)
+            green = (entries[1] * GREEN_STEPS + 0.5).astype(jnp.int32)
+            pairs[k, parity] = red * 65536 + green
+            for c in (2, 3):
+                bins[k, c - 2, parity] = entries[c]
 
     for rel in (r1, r2):
         @pl.when(d == 0)
@@ -228,13 +236,18 @@
         for h in range(2):
             store_relaxed(r2, z, t, h, collide(f[h], fluids[h], WALL_REST[1]))
 
-    def lookup(c, parity, index, tags):
-        picked = [
-            jnp.take_along_axis(bins[k, c, parity], index, axis=1, mode="promise_in_bounds") for k in range(4)
-        ]
+    def lookup(tables, index, tags):
+        picked = [jnp.take_along_axis(each, index, axis=1, mode="promise_in_bounds") for each in tables]
         return jnp.where(
             tags[0], jnp.where(tags[1], picked[3], picked[2]), jnp.where(tags[1], picked[1], picked[0])
         )
+
+    def lookup_pair(parity, index, tags):
+        word = lookup([pairs[k, parity] for k in range(4)], index, tags)
+        return (word >> 16).astype(F32), (word & 65535).astype(F32)
+
+    def lookup_one(c, parity, index, tags):
+        return lookup([bins[k, c - 2, parity] for k in range(4)], index, tags)
 
     def classify(z, t, places):
         rows = pl.ds(pl.multiple_of(8 * t, 8), 8)
@@ -250,10 +263,16 @@
                 even, odd = (lower + 1) >> 1, lower >> 1
                 place.append((1.0 - jnp.abs(where - (even + even).astype(F32)), even, odd))
             result = []
-            for (share, even, odd), channels in zip(place, ((0, 1, 2), (3,))):
-                at_odd = [lookup(c, 1, odd, tags) for c in channels]
-                at_even = [lookup(c, 0, even, tags) for c in channels]
+            for (share, even, odd), c in zip(place, (2, 3)):
+                at_odd = [lookup_one(c, 1, odd, tags)]
+                if c == 2:
+                    at_odd += lookup_pair(1, odd, tags)
+                at_even = [lookup_one(c, 0, even, tags)]
+                if c == 2:
+                    at_even += lookup_pair(0, even, tags)
                 result += [a + share * (b - a) for a, b in zip(at_odd, at_even)]
+            blue, red, green, opacity = result
+            result = [red * (1.0 / RED_STEPS), green * (1.0 / GREEN_STEPS), blue, opacity]
             coverage = jnp.where(fluids[h], result[3] * (3.0 / (NZL * ND)), 0.0)
             for c in range(3):
                 cbuf[c, z, padded, lanes] = result[c] * coverage
@@ -523,10 +542,10 @@
         return carry
 
     unpack_sites(0, (1, 2, 3, 4))
-    lax.fori_loop(0, 4, columns_inner, 0)
+    lax.fori_loop(0, 4, columns_inner, 0, unroll=2)
     render(0, (1, 2, 3, 4))
     unpack_sites(1, (0, 5))
-    lax.fori_loop(0, 2, columns_outer, 0)
+    lax.fori_loop(0, 2, columns_outer, 0, unroll=2)
 
     partner = at(d + 1 - 2 * core, r)
     swaps = [
@@ -616,7 +635,8 @@
             pltpu.VMEM((2, 2, 64, 128), F32),
             pltpu.VMEM((2, 4, 8, 128), F32),
             pltpu.VMEM((2, 4, 8, 128), F32),
-            pltpu.VMEM((4, 4, 2, 8, 128), F32),
+            pltpu.VMEM((4, 2, 2, 8, 128), F32),
+            pltpu.VMEM((4, 2, 8, 128), jnp.int32),
             pltpu.VMEM((4, NZL, 48, NX), F32),
             pltpu.VMEM((2, 3, 8, NX), F32),
             pltpu.VMEM((2, 3, 8, NX), F32),

time: 40.3 us -> 39.6 us (0.983)
  Pallas kernels: 39.4 us -> 38.8 us
    pallas_call x1, Pallas kernels: 37.5 us -> 36.9 us  [shards(): pl.pallas_call(kernel, out_shape=(pltpu.VMEM(populations.shape, F32), plt...]
where the time goes in v5:
time: 39.6 us; the launch traced here: 39.5 us
  Pallas kernels  38.8 us (98%)
  between operations  0.64 us (2%)
    pallas_call x1, Pallas kernels, shards(): pl.pallas_call(kernel, out_shape=(pltpu.VMEM(populations.shape, F32), plt...  36.9 us
    pallas_call x1, Pallas kernels, shards(): pl.pallas_call(deliver, out_shape=(jax.ShapeDtypeStruct(populations.shape...  1.92 us

profile of v5, /device:TPU:0, one launch (start us, length us, event | category | flops | bytes accessed | tf_op | source)
XLA Modules:
  0.0 39.5 jit_solution(3330652518643724882)
XLA Ops:
  0.6 36.9 %vessel.1 = (f32[19,6,32,256]{3,2,1,0:T(8,128)S(1)}, f32[4,4,512]{2,1,0:T(4,128)S(1)}) custom-call(f32[19,6,32,256]{3,2,1,0:T(8,128)} %pops.1, s32[6,32,256]{2,1,0:T(8,128)} %mask_in.1, s32[6,32,256]{2,1,0:T(8,128)} %tag_in.1, f32[4,4,256]{2,1,0:T(4,128)} %table.1), custom_call_target="tpu_custom_call" | custom-call | tf_op jit(solution)/shard_map/vessel/pallas_call | solution.py:621
  37.6 1.9 %deliver.1 = (f32[19,6,32,256]{3,2,1,0:T(8,128)}, f32[4,4,512]{2,1,0:T(4,128)}) custom-call(f32[19,6,32,256]{3,2,1,0:T(8,128)S(1)} %get-tuple-element.4.advanced, f32[4,4,512]{2,1,0:T(4,128)S(1)} %get-tuple-element.5.drawn), custom_call_target="tpu_custom_call" | custom-call | tf_op jit(solution)/shard_map/deliver/pallas_call | solution.py:660

commit v6 on v5

--- a/solution.py
+++ b/solution.py
@@ -123,14 +123,17 @@
     peers += columns_peers
     peers += [at(2 * (row_first + lax.rem(chip + k, 4)) + core, r) for k in (2, 1, 3)]
     peers += [at(up_d, r), at(down_d, r), at(d, up_r), at(d, down_r), at(d + 1 - 2 * core, r)]
-    for peer in peers:
-        pl.semaphore_signal(barrier, inc=1, device_id=peer, device_id_type=MESH)
-
     loads = [pltpu.make_async_copy(pops.at[:, z], pbuf.at[:, z], in_sem.at[z]) for z in range(NZL)]
     loads.append(pltpu.make_async_copy(mask_in, mask, in_sem.at[NZL]))
     loads.append(pltpu.make_async_copy(tag_in, tag, in_sem.at[NZL + 1]))
-    for n in (NZL, 0, 5, 1, 2, 3, 4, NZL + 1):
+    for n in (NZL, 5, 0):
         loads[n].start()
+
+    for peer in peers:
+        pl.semaphore_signal(barrier, inc=1, device_id=peer, device_id_type=MESH)
+    for n in (1, 2, 3, 4, NZL + 1):
+        loads[n].start()
+
 
     lane = lax.broadcasted_iota(jnp.int32, (8, 128), 1)
     first_lane, last_lane = lane == 0, lane == 127
@@ -392,9 +395,10 @@
                 rel[POS[q], layer, h, row:row + 1, :] = jnp.where(edges[n], WALL, crecv[s, n, h:h + 1, :])
 
     loads[NZL].wait()
-    loads[0].wait()
-    loads[5].wait()
-    outer_tiles(first_tile, None, None)
+    for z in (5, 0):
+        loads[z].wait()
+        for t in range(4):
+            first_tile(z, t)
     pack_corners(0, r1)
     pl.semaphore_wait(barrier, len(peers))
     layers1 = [copy for t in range(4) for copy in layer_copies(0, r1, t)]

time: 39.6 us -> 39.6 us (level)
  no operation moved by 1% of the time
where the time goes in v6:
time: 39.6 us; the launch traced here: 39.5 us
  Pallas kernels  38.8 us (98%)
  between operations  0.64 us (2%)
    pallas_call x1, Pallas kernels, shards(): pl.pallas_call(kernel, out_shape=(pltpu.VMEM(populations.shape, F32), plt...  36.9 us
    pallas_call x1, Pallas kernels, shards(): pl.pallas_call(deliver, out_shape=(jax.ShapeDtypeStruct(populations.shape...  1.92 us

profile of v6, /device:TPU:0, one launch (start us, length us, event | category | flops | bytes accessed | tf_op | source)
XLA Modules:
  0.0 39.5 jit_solution(15891968316206611392)
XLA Ops:
  0.6 36.9 %vessel.1 = (f32[19,6,32,256]{3,2,1,0:T(8,128)S(1)}, f32[4,4,512]{2,1,0:T(4,128)S(1)}) custom-call(f32[19,6,32,256]{3,2,1,0:T(8,128)} %pops.1, s32[6,32,256]{2,1,0:T(8,128)} %mask_in.1, s32[6,32,256]{2,1,0:T(8,128)} %tag_in.1, f32[4,4,256]{2,1,0:T(4,128)} %table.1), custom_call_target="tpu_custom_call" | custom-call | tf_op jit(solution)/shard_map/vessel/pallas_call | solution.py:625
  37.5 1.9 %deliver.1 = (f32[19,6,32,256]{3,2,1,0:T(8,128)}, f32[4,4,512]{2,1,0:T(4,128)}) custom-call(f32[19,6,32,256]{3,2,1,0:T(8,128)S(1)} %get-tuple-element.4.advanced, f32[4,4,512]{2,1,0:T(4,128)S(1)} %get-tuple-element.5.drawn), custom_call_target="tpu_custom_call" | custom-call | tf_op jit(solution)/shard_map/deliver/pallas_call | solution.py:664
